TPU v7x, 32 devices: a whole 2x2x4 slice. The times are simulated.
32 devices in a mesh: dom: 8 (over z, y), batch: 4 (over x, core).
Axes of the slice: x: 2, y: 2, z: 4, core: 2. Of those that a mesh axis runs over, the one named last changes fastest.
Arguments:
- signal: bfloat16 [4096, 4, 4, 256], P('dom', 'batch'), may hold values from -6 to 6
- cotangent: bfloat16 [4096, 4, 3, 256], P('dom', 'batch'), may hold values from -6 to 6
- conv_weight: bfloat16 [2, 2, 256, 256], replicated, may hold values from -0.25 to 0.25
- mix_weight: bfloat16 [3, 256, 256], replicated, may hold values from -0.21875 to 0.21875
- send_rows: int32 [64, 16], P('dom'), may hold values from 0 to 511
- send_mask: int32 [64, 16], P('dom'), may hold values 0 or 1
- tile_vals: bfloat16 [128, 128, 128], P('dom'), may hold values from -0.26953125 to 0.26953125
- tile_row: int32 [128], P('dom'), may hold values from 0 to 3
- tile_col: int32 [128], P('dom'), may hold values from 0 to 5
- tile_mask: int32 [128], P('dom'), may hold values 0 or 1
- hub_owner: int32 [8], replicated, may hold values from 0 to 7, as said below
- hub_rows: int32 [8, 16], replicated, may hold values from 0 to 511
Outputs:
- layer_out: bfloat16 [4096, 4, 3, 256], P('dom', 'batch')
- signal_grad: bfloat16 [4096, 4, 4, 256], P('dom', 'batch')
- conv_grad: float32 [2, 2, 256, 256], replicated
- mix_grad: float32 [3, 256, 256], replicated
Inputs may be any that keep to these rules, and one draw needn't show every extreme that they name: `hub_owner`: each owner slot names a different partition.
All inputs are finite; a program needn't handle non-finite values. No bound on the sum of `send_mask` or of `tile_mask` on one device may be relied on, other than what follows from the above.
Results may differ from a plain program's by a relative error of at most 0.0056.
Values may be sent and summed in bfloat16 or wider, within the bound.
A program may use at most 128 MiB of HBM per device.

v0:
```python
import functools
import math

import jax
import jax.numpy as jnp
import numpy as np
from jax import lax
from jax.experimental import pallas as pl
from jax.experimental.pallas import tpu as pltpu
from jax.sharding import PartitionSpec as P

VMEM = pl.BlockSpec(memory_space=pltpu.VMEM)
SMEM = pl.BlockSpec(memory_space=pltpu.SMEM)
F32 = jnp.float32
BF16 = jnp.bfloat16


def nn(left, right):
    return lax.dot_general(left, right, (((1,), (0,)), ((), ())), preferred_element_type=F32)


def nt(left, right):
    return lax.dot_general(left, right, (((1,), (1,)), ((), ())), preferred_element_type=F32)


def tn(left, right):
    return lax.dot_general(left, right, (((0,), (0,)), ((), ())), preferred_element_type=F32)


def fill_taps(conv_ref, taps_ref):
    chans = conv_ref.shape[2]
    for kind in range(2):
        for tap in range(2):
            taps_ref[tap * chans : (tap + 1) * chans, kind * chans : (kind + 1) * chans] = conv_ref[
                kind, tap
            ]


def pre_kernel(
    row_ref,
    col_ref,
    keep_ref,
    sig_ref,
    cot_ref,
    conv_ref,
    mix_ref,
    tile_ref,
    owner_ref,
    rows_ref,
    flag_ref,
    hubs_ref,
    expand_ref,
    lane_ref,
    halo_ref,
    own_ref,
    far_ref,
    send_ref,
    hidden_ref,
    tanh_ref,
    gate_ref,
    back_ref,
    out_ref,
    dense_ref,
    place_ref,
    taps_ref,
):
    nodes = own_ref.shape[0]
    tiles, block, _ = tile_ref.shape
    chans = conv_ref.shape[2]
    features = hidden_ref.shape[1]
    own_tiles = nodes // block
    all_tiles = dense_ref.shape[0]

    dense_ref[...] = jnp.zeros_like(dense_ref)
    for t in range(tiles):

        @pl.when(keep_ref[t] == 1)
        def _():
            rows = pl.ds(pl.multiple_of(row_ref[t] * block, block), block)
            dense_ref[col_ref[t], rows, :] += tile_ref[t].astype(F32)

    for c in range(own_tiles):
        own_ref[:, c * block : (c + 1) * block] = dense_ref[c].astype(BF16)
    slots = send_ref.shape[0]
    cap = rows_ref.shape[1]
    groups, hub_per = hubs_ref.shape
    width = slots // expand_ref.shape[1]
    halo = halo_ref.shape[0]
    place_ref[:halo, :] = halo_ref[...]
    slot = lax.broadcasted_iota(jnp.int32, (hub_per, slots), 1)
    entry = lax.broadcasted_iota(jnp.int32, (hub_per, slots), 0) + cap
    me = lax.axis_index("dom")
    hub = jnp.zeros((1, hub_per), F32)
    for o in range(groups):
        at = halo + o * hub_per
        owner = owner_ref[o]
        place_ref[at : at + hub_per, :] = jnp.where(slot == entry + owner * width, 1.0, 0.0).astype(
            BF16
        )
        owned = (owner == me).astype(F32)
        hub += owned * (hubs_ref[o : o + 1, :].astype(F32) + 1.0)
    far = nn(dense_ref[own_tiles].astype(BF16), place_ref[:block, :])
    for c in range(own_tiles + 1, all_tiles):
        at = (c - own_tiles) * block
        far += nn(dense_ref[c].astype(BF16), place_ref[at : at + block, :])
    far_ref[...] = far.astype(BF16)
    chosen = jnp.where(flag_ref[...] == 1, rows_ref[...].astype(F32) + 1.0, 0.0)
    spread = jnp.dot(
        expand_ref[...], chosen, precision=lax.Precision.HIGHEST, preferred_element_type=F32
    )
    lane = lane_ref[...]
    from_halo = jnp.where(
        lax.broadcasted_iota(jnp.int32, (slots, cap), 1) == lane, spread, 0.0
    )
    from_hub = jnp.where(
        lax.broadcasted_iota(jnp.int32, (slots, hub_per), 1) + cap == lane,
        jnp.broadcast_to(hub, (slots, hub_per)),
        0.0,
    )
    pick = jnp.sum(from_halo, axis=1, keepdims=True) + jnp.sum(from_hub, axis=1, keepdims=True)
    pick = (pick + 0.5).astype(jnp.int32) - 1
    send_ref[...] = jnp.where(
        pick == lax.broadcasted_iota(jnp.int32, (slots, nodes), 1), 1.0, 0.0
    ).astype(BF16)

    fill_taps(conv_ref, taps_ref)
    for t in range(features // chans):
        at = slice(t * chans, (t + 1) * chans)
        both = nn(sig_ref[:, t * chans : (t + 2) * chans], taps_ref[...])
        tanh_filt = jnp.tanh(both[:, :chans])
        sig_gate = jax.nn.sigmoid(both[:, chans:])
        tanh_ref[:, at] = tanh_filt
        gate_ref[:, at] = sig_gate
        hidden_ref[:, at] = (tanh_filt * sig_gate).astype(BF16)
        back_ref[:, at] = nt(cot_ref[t], mix_ref[2]).astype(BF16)
    out_ref[:, :features] = nn(send_ref[...], hidden_ref[...]).astype(BF16)
    out_ref[:, features:] = tn(far_ref[...], back_ref[...]).astype(BF16)


def rows_of(index, width):
    return pl.ds(pl.multiple_of(index * width, 16), width)


def exchange(devices, out_ref, in_ref, send_sem, recv_sem):
    slots, lanes = out_ref.shape
    width = slots // devices
    half = lanes // 2
    me = lax.axis_index("dom")
    barrier = pltpu.get_barrier_semaphore()
    for d in range(1, devices):
        pl.semaphore_signal(
            barrier,
            inc=1,
            device_id={"dom": lax.rem(me + d, devices)},
            device_id_type=pl.DeviceIdType.MESH,
        )
    pl.semaphore_wait(barrier, devices - 1)
    groups = []
    for k, span in enumerate((slice(half, lanes), slice(0, half))):
        copies = []
        for d in range(1, devices):
            other = lax.rem(me + d, devices)
            copy = pltpu.make_async_remote_copy(
                src_ref=out_ref.at[rows_of(other, width), span],
                dst_ref=in_ref.at[rows_of(me, width), span],
                send_sem=send_sem.at[k, d - 1],
                recv_sem=recv_sem.at[k, d - 1],
                device_id={"dom": other},
                device_id_type=pl.DeviceIdType.MESH,
            )
            copy.start()
            copies.append(copy)
        groups.append(copies)
    in_ref[rows_of(me, width), :] = out_ref[rows_of(me, width), :]
    return groups


def mid_kernel(
    devices,
    own_ref,
    far_ref,
    send_ref,
    hidden_ref,
    back_ref,
    cot_ref,
    mix_ref,
    leave_ref,
    hop_ref,
    next_ref,
    out_ref,
    in_ref,
    hop_sum,
    next_sum,
    send_sem,
    recv_sem,
):
    features = hidden_ref.shape[1]
    chans = mix_ref.shape[1]
    spans = [slice(t * chans, (t + 1) * chans) for t in range(features // chans)]
    late, early = exchange(devices, leave_ref, in_ref, send_sem, recv_sem)
    for t, at in enumerate(spans):
        next_sum[:, at] = nt(cot_ref[t], mix_ref[1]) + tn(own_ref[...], back_ref[:, at])
        hop_sum[:, at] = nn(own_ref[...], hidden_ref[:, at])
    for copy in late:
        copy.wait_recv()
    next_ref[...] = (next_sum[...] + tn(send_ref[...], in_ref[:, features:])).astype(BF16)
    out_ref[:, features:] = tn(far_ref[...], next_ref[...]).astype(BF16)
    for copy in early:
        copy.wait_recv()
    hop_ref[...] = (hop_sum[...] + nn(far_ref[...], in_ref[:, :features])).astype(BF16)
    out_ref[:, :features] = nn(send_ref[...], hop_ref[...]).astype(BF16)
    for copy in late + early:
        copy.wait_send()


def post_kernel(
    devices,
    own_ref,
    far_ref,
    send_ref,
    hidden_ref,
    hop_ref,
    back_ref,
    leave_ref,
    sig_ref,
    cot_ref,
    tanh_ref,
    gate_ref,
    conv_ref,
    mix_ref,
    layer_ref,
    grad_ref,
    weight_ref,
    in_ref,
    hop_sum,
    layer_sum,
    hidden_sum,
    taps_ref,
    last_ref,
    held_ref,
    send_sem,
    recv_sem,
):
    features = hidden_ref.shape[1]
    chans = mix_ref.shape[1]
    spans = [slice(t * chans, (t + 1) * chans) for t in range(features // chans)]
    late, early = exchange(devices, leave_ref, in_ref, send_sem, recv_sem)

    def add_weight(spot, part, first):
        place = slice(spot * chans, (spot + 1) * chans)
        weight_ref[place, :] = part if first else weight_ref[place, :] + part

    fill_taps(conv_ref, taps_ref)
    for t, at in enumerate(spans):
        hidden_sum[:, at] = nt(cot_ref[t], mix_ref[0]) + tn(own_ref[...], back_ref[:, at])
        hop_sum[:, at] = nn(own_ref[...], hop_ref[:, at])
        layer_sum[:, at] = (
            sig_ref[:, (t + 1) * chans : (t + 2) * chans].astype(F32)
            + nn(hidden_ref[:, at], mix_ref[0])
            + nn(hop_ref[:, at], mix_ref[1])
        )
        add_weight(4, tn(hidden_ref[:, at], cot_ref[t]), t == 0)
        add_weight(5, tn(hop_ref[:, at], cot_ref[t]), t == 0)

    for copy in late:
        copy.wait_recv()
    for t, at in enumerate(spans):
        cot = cot_ref[t]
        grad_hidden = hidden_sum[:, at] + tn(
            send_ref[...], in_ref[:, features + t * chans : features + (t + 1) * chans]
        )
        tanh_filt = tanh_ref[:, at]
        sig_gate = gate_ref[:, at]
        held_ref[:, :chans] = (
            grad_hidden * sig_gate * (1.0 - tanh_filt * tanh_filt)
        ).astype(BF16)
        held_ref[:, chans:] = (grad_hidden * tanh_filt * sig_gate * (1.0 - sig_gate)).astype(BF16)
        outer = tn(sig_ref[:, t * chans : (t + 2) * chans], held_ref[...])
        for kind in range(2):
            for tap in range(2):
                part = outer[tap * chans : (tap + 1) * chans, kind * chans : (kind + 1) * chans]
                add_weight(kind * 2 + tap, part, t == 0)
        into = nt(held_ref[...], taps_ref[...])
        before = into[:, :chans]
        if t > 0:
            before = before + carried
        grad_ref[:, at] = before.astype(BF16)
        carried = into[:, chans:] + cot.astype(F32)
    grad_ref[:, features:] = carried.astype(BF16)

    for copy in early:
        copy.wait_recv()
    for t, at in enumerate(spans):
        last_ref[...] = (hop_sum[:, at] + nn(far_ref[...], in_ref[:, at])).astype(BF16)
        layer_ref[t] = (layer_sum[:, at] + nn(last_ref[...], mix_ref[2])).astype(BF16)
        add_weight(6, tn(last_ref[...], cot_ref[t]), t == 0)
    for copy in late + early:
        copy.wait_send()


def pairs_of(axis, size):
    stages, stride = [], 1
    while stride < size:
        stages.append((axis, stride, 2))
        stride *= 2
    return stages


def plan_of(order, rows):
    plan, count = [], rows
    for axis, stride, size in order:
        split = count % (size * 16) == 0
        if split:
            count //= size
        plan.append((axis, stride, size, split, count))
    return plan


def colours_of(axis_sizes, rows, chans):
    sizes = dict(axis_sizes)
    batch = pairs_of("batch", sizes["batch"])
    first, rest = batch[:1], batch[1:]
    direct = [("dom", 1, sizes["dom"])]
    pairs = pairs_of("dom", sizes["dom"])
    share = (rows // chans + 1) // 2 * chans
    for middle in (direct, pairs):
        colours = [
            (0, share, plan_of(first + rest + middle, share)),
            (share, rows - share, plan_of(first + middle + rest, rows - share)),
        ]
        if all(split or size == 2 for _, _, plan in colours for _, _, size, split, _ in plan):
            break
    return colours


def narrow(stage, split):
    return split and stage in (1, 2)


def landing_rows(colours, wanted):
    return sum(
        count * (size - 1)
        for _, _, plan in colours
        for stage, (_, _, size, split, count) in enumerate(plan)
        if narrow(stage, split) == wanted
    )


def others_of(axis, stride, size):
    index = lax.axis_index(axis)
    place = lax.rem(lax.div(index, stride), size)
    base = index - place * stride
    seats = [lax.rem(place + d, size) for d in range(1, size)]
    return place, [(seat, base + seat * stride) for seat in seats]


def reduce_kernel(
    colours,
    factor,
    grads_ref,
    out_ref,
    total,
    wide,
    landed,
    leaving,
    send_sem,
    recv_sem,
    back_send,
    back_recv,
):
    barrier = pltpu.get_barrier_semaphore()
    peers = sorted({(axis, stride, size) for axis, stride, size, _, _ in colours[0][2]})
    for axis, stride, size in peers:
        for _, other in others_of(axis, stride, size)[1]:
            pl.semaphore_signal(
                barrier, inc=1, device_id={axis: other}, device_id_type=pl.DeviceIdType.MESH
            )
    pl.semaphore_wait(barrier, sum(size - 1 for _, _, size in peers))

    starts = [base for base, _, _ in colours]
    trail = [[] for _ in colours]
    used = {True: 0, False: 0}
    depth = len(colours[0][2])
    for s in range(depth):
        moves = []
        for c, (_, _, plan) in enumerate(colours):
            axis, stride, size, split, count = plan[s]
            small = narrow(s, split)
            landing = landed if small else wide
            place, others = others_of(axis, stride, size)
            source = grads_ref if s == 0 else total
            keep = starts[c] + place * count if split else starts[c]
            keep_rows = pl.ds(pl.multiple_of(keep, 16), count)
            arrivals = []
            for d, (seat, other) in enumerate(others):
                give = starts[c] + seat * count if split else starts[c]
                give_rows = pl.ds(pl.multiple_of(give, 16), count)
                spot = pl.ds(used[small], count)
                if small:
                    leaving[spot, :] = source[give_rows, :].astype(BF16)
                copy = pltpu.make_async_remote_copy(
                    src_ref=leaving.at[spot] if small else source.at[give_rows],
                    dst_ref=landing.at[spot],
                    send_sem=send_sem.at[c, s, d],
                    recv_sem=recv_sem.at[c, s, d],
                    device_id={axis: other},
                    device_id_type=pl.DeviceIdType.MESH,
                )
                copy.start()
                arrivals.append((copy, spot))
                used[small] += count
            moves.append((arrivals, landing, source, keep_rows))
            trail[c].append(keep)
            starts[c] = keep
        for arrivals, landing, source, keep_rows in moves:
            for copy, _ in arrivals:
                copy.wait()
            value = source[keep_rows, :]
            for _, spot in arrivals:
                value = value + landing[spot, :].astype(F32)
            total[keep_rows, :] = value

    for c, (_, _, plan) in enumerate(colours):
        rows = pl.ds(pl.multiple_of(starts[c], 16), plan[-1][4])
        out_ref[rows, :] = (total[rows, :] * factor).astype(BF16)
    for s in range(depth - 1, -1, -1):
        moves = []
        for c, (_, _, plan) in enumerate(colours):
            axis, stride, size, split, count = plan[s]
            if not split:
                continue
            rows = pl.ds(pl.multiple_of(trail[c][s], 16), count)
            for d, (_, other) in enumerate(others_of(axis, stride, size)[1]):
                copy = pltpu.make_async_remote_copy(
                    src_ref=out_ref.at[rows],
                    dst_ref=out_ref.at[rows],
                    send_sem=back_send.at[c, s, d],
                    recv_sem=back_recv.at[c, s, d],
                    device_id={axis: other},
                    device_id_type=pl.DeviceIdType.MESH,
                )
                copy.start()
                moves.append(copy)
        for copy in moves:
            copy.wait()


def reduce_weights(grads, axis_sizes, factor, chans):
    rows, lanes = grads.shape
    colours = colours_of(axis_sizes, rows, chans)
    most = max(size for _, _, size, _, _ in colours[0][2]) - 1
    sems = pltpu.SemaphoreType.DMA((len(colours), len(colours[0][2]), most))
    slim = landing_rows(colours, True)
    return pl.pallas_call(
        functools.partial(reduce_kernel, colours, factor),
        out_shape=jax.ShapeDtypeStruct((rows, lanes), BF16),
        in_specs=[VMEM],
        out_specs=VMEM,
        scratch_shapes=[
            pltpu.VMEM((rows, lanes), F32),
            pltpu.VMEM((landing_rows(colours, False), lanes), F32),
            pltpu.VMEM((slim, lanes), BF16),
            pltpu.VMEM((slim, lanes), BF16),
            sems,
            sems,
            sems,
            sems,
        ],
        compiler_params=pltpu.CompilerParams(collective_id=0, has_side_effects=True),
        name="reduce_weights",
    )(grads)


def shape_of(*dims, dtype=BF16):
    return jax.ShapeDtypeStruct(dims, dtype)


def body(
    axis_sizes,
    signal,
    cotangent,
    conv_weight,
    mix_weight,
    send_rows,
    send_mask,
    tile_vals,
    tile_row,
    tile_col,
    tile_mask,
    hub_owner,
    hub_rows,
):
    nodes, b_dev, steps, chans = signal.shape
    out_steps = steps - 1
    features = out_steps * chans
    n_dom, cap = send_rows.shape
    hub_per = hub_rows.shape[1]
    width = -(-(cap + hub_per) // 16) * 16
    slots = n_dom * width
    block = tile_vals.shape[1]
    all_tiles = (nodes + n_dom * cap + hub_rows.size) // block

    sig = signal.reshape(nodes, steps * chans)
    cot = jnp.transpose(cotangent.reshape(nodes, out_steps, chans), (1, 0, 2))

    slot = np.arange(slots)
    expand = (slot[:, None] // width == np.arange(n_dom)[None, :]).astype(np.float32)
    lane = (slot % width).astype(np.int32)[:, None]
    entry = np.arange(n_dom * cap)
    halo = jnp.asarray(
        (entry // cap * width + entry % cap)[:, None] == slot[None, :], dtype=BF16
    )

    own, far, send, hidden, tanh_filt, sig_gate, back_two, out_one = pl.pallas_call(
        pre_kernel,
        out_shape=(
            shape_of(nodes, nodes),
            shape_of(nodes, slots),
            shape_of(slots, nodes),
            shape_of(nodes, features),
            shape_of(nodes, features, dtype=F32),
            shape_of(nodes, features, dtype=F32),
            shape_of(nodes, features),
            shape_of(slots, 2 * features),
        ),
        in_specs=[SMEM] * 3 + [VMEM] * 5 + [SMEM] + [VMEM] * 6,
        out_specs=(VMEM,) * 8,
        scratch_shapes=[
            pltpu.VMEM((all_tiles, nodes, block), F32),
            pltpu.VMEM((n_dom * cap + hub_rows.size, slots), BF16),
            pltpu.VMEM((2 * chans, 2 * chans), BF16),
        ],
        name="pre",
    )(
        tile_row,
        tile_col,
        tile_mask,
        sig,
        cot,
        conv_weight,
        mix_weight,
        tile_vals,
        hub_owner,
        send_rows,
        send_mask,
        hub_rows,
        expand,
        lane,
        halo,
    )

    sems = pltpu.SemaphoreType.DMA((2, n_dom - 1))
    landing = pltpu.VMEM((slots, 2 * features), BF16)
    partial = pltpu.VMEM((nodes, features), F32)
    hop_one, back_one, out_two = pl.pallas_call(
        functools.partial(mid_kernel, n_dom),
        out_shape=(
            shape_of(nodes, features),
            shape_of(nodes, features),
            shape_of(slots, 2 * features),
        ),
        in_specs=[VMEM] * 8,
        out_specs=(VMEM,) * 3,
        scratch_shapes=[landing, partial, partial, sems, sems],
        compiler_params=pltpu.CompilerParams(collective_id=1, has_side_effects=True),
        name="mid",
    )(own, far, send, hidden, back_two, cot, mix_weight, out_one)
    layer_out, signal_grad, grads = pl.pallas_call(
        functools.partial(post_kernel, n_dom),
        out_shape=(
            shape_of(out_steps, nodes, chans),
            shape_of(nodes, steps * chans),
            shape_of(7 * chans, chans, dtype=F32),
        ),
        in_specs=[VMEM] * 13,
        out_specs=(VMEM,) * 3,
        scratch_shapes=[
            landing,
            partial,
            partial,
            partial,
            pltpu.VMEM((2 * chans, 2 * chans), BF16),
            pltpu.VMEM((nodes, chans), BF16),
            pltpu.VMEM((nodes, 2 * chans), BF16),
            sems,
            sems,
        ],
        compiler_params=pltpu.CompilerParams(collective_id=2, has_side_effects=True),
        name="post",
    )(
        own,
        far,
        send,
        hidden,
        hop_one,
        back_one,
        out_two,
        sig,
        cot,
        tanh_filt,
        sig_gate,
        conv_weight,
        mix_weight,
    )
    total_count = nodes * out_steps * b_dev
    for _, size in axis_sizes:
        total_count *= size
    reduced = reduce_weights(grads, axis_sizes, 1.0 / math.sqrt(total_count), chans)
    return (
        jnp.transpose(layer_out, (1, 0, 2)).reshape(nodes, b_dev, out_steps, chans),
        signal_grad.reshape(signal.shape),
        reduced[: 4 * chans].astype(F32).reshape(conv_weight.shape),
        reduced[4 * chans :].astype(F32).reshape(mix_weight.shape),
    )


def solution(mesh):
    placed = (
        P("dom", "batch", None, None),
        P("dom", "batch", None, None),
        P(),
        P(),
        P("dom", None),
        P("dom", None),
        P("dom", None, None),
        P("dom"),
        P("dom"),
        P("dom"),
        P(),
        P(),
    )
    axis_sizes = tuple((axis, mesh.shape[axis]) for axis in ("dom", "batch"))
    return jax.shard_map(
        functools.partial(body, axis_sizes),
        mesh=mesh,
        in_specs=placed,
        out_specs=(P("dom", "batch", None, None), P("dom", "batch", None, None), P(), P()),
        check_vma=False,
    )
```

profile of v0, /device:TPU:0, one launch (start us, length us, event | category | flops | bytes accessed | tf_op | source)
XLA Modules:
  0.0 102.4 jit_solution(17567077964086703652)
XLA Ops:
  0.6 2.4 %copy.20 = bf16[64,8,4,256]{3,1,2,0:T(8,128)(2,1)} copy(bf16[64,8,4,256]{3,2,1,0:T(4,128)(2,1)} %bitcast.21) | data formatting | bytes 2097152
  3.1 6.3 %pre.1 = (bf16[512,512]{1,0:T(8,128)(2,1)}, bf16[512,256]{1,0:T(8,128)(2,1)}, bf16[256,512]{1,0:T(8,128)(2,1)}, bf16[512,768]{1,0:T(8,128)(2,1)}, f32[512,768]{1...) custom-call(s32[16]{0:T(128)} %row_ref.1, s32[16]{0:T(128)} %col_ref.1, ...), custom_call_target="tpu_custom_call" | custom-call | tf_op jit(solution)/shard_map/pre/pallas_call | solution.py:514
  9.4 25.4 %mid.1 = (bf16[512,768]{1,0:T(8,128)(2,1)}, bf16[512,768]{1,0:T(8,128)(2,1)}, bf16[256,1536]{1,0:T(8,128)(2,1)}) custom-call(bf16[512,512]{1,0:T(8,128)(2,1)} %get-tuple-element.18.own_ref, bf16[512,256]{1,0:T(8,128)(2,1)} %get-tuple-element.19.far_ref, bf16[256,512]{1,0:T(8,128)(2,1)} %get-tuple-element.20.send_ref, ...), custom_call_target="tpu_custom_call" | custom-call | tf_op jit(solution)/shard_map/mid/pallas_call | solution.py:555
  34.8 28.5 %post.1 = (bf16[3,512,256]{2,1,0:T(8,128)(2,1)}, bf16[512,1024]{1,0:T(8,128)(2,1)}, f32[1792,256]{1,0:T(8,128)}) custom-call(bf16[512,512]{1,0:T(8,128)(2,1)} %get-tuple-element.18.own_ref, bf16[512,256]{1,0:T(8,128)(2,1)} %get-tuple-element.19.far_ref, bf16[256,512]{1,0:T(8,128)(2,1)} %get-tuple-element.20.send_ref, ...), custom_call_target="tpu_custom_call" | custom-call | tf_op jit(solution)/shard_map/post/pallas_call | solution.py:568
  63.3 33.7 %reduce_weights.1 = bf16[1792,256]{1,0:T(8,128)(2,1)} custom-call(f32[1792,256]{1,0:T(8,128)} %get-tuple-element.31.grads_ref), custom_call_target="tpu_custom_call" | custom-call | tf_op jit(solution)/shard_map/reduce_weights/pallas_call | solution.py:454
  96.9 0.0 slice-start
  96.9 0.0 slice-start.1
  97.0 0.0 copy-start
  97.0 1.0 slice-done
  97.9 0.9 convert.3
  98.9 0.0 slice-done.1
  98.9 0.0 copy-start.1
  98.9 1.1 %convert.2 = f32[2,2,256,256]{3,2,1,0:T(8,128)} convert(bf16[2,2,256,256]{3,2,1,0:T(8,128)(2,1)S(1)} %bitcast.20) | non-fusion elementwise | flops 262144 | bytes 1572864 | tf_op jit(solution)/shard_map/reshape | solution.py:612
  99.9 0.0 copy-done
  99.9 1.6 %reshape.35 = bf16[512,1,4,256]{3,2,0,1:T(4,128)(2,1)} reshape(bf16[512,1024]{1,0:T(8,128)(2,1)S(1)} %copy-done) | data formatting | bytes 2097152 | tf_op jit(solution)/shard_map/reshape | solution.py:611
  101.5 0.0 copy-done.1
  101.5 0.9 copy.22
Async XLA Ops:
  96.9 1.0 slice-start
  96.9 1.9 %slice-start.1 = ((bf16[1792,256]{1,0:T(8,128)(2,1)}), bf16[1024,256]{1,0:T(8,128)(2,1)S(1)}, s32[]{:S(2)}) async-start(bf16[1792,256]{1,0:T(8,128)(2,1)} %reduce_weights.1), calls=%async_computation.1 | async-start | bytes 1048576 | tf_op jit(solution)/shard_map/slice | solution.py:612
  97.0 3.0 %copy-start = (bf16[512,1024]{1,0:T(8,128)(2,1)S(1)}, bf16[512,1024]{1,0:T(8,128)(2,1)}, u32[]{:S(2)}) copy-start(bf16[512,1024]{1,0:T(8,128)(2,1)} %get-tuple-element.30) | copy-start | bytes 3145732
  98.9 2.6 %copy-start.1 = (bf16[3,512,256]{2,1,0:T(8,128)(2,1)S(1)}, bf16[3,512,256]{2,1,0:T(8,128)(2,1)}, u32[]{:S(2)}) copy-start(bf16[3,512,256]{2,1,0:T(8,128)(2,1)} %get-tuple-element.29) | copy-start | bytes 2359300
where the time goes:
time: 103 us; the launch traced here: 102 us
  Pallas kernels  93.9 us (91%)
  local copies, waits for them, and re-layouts  5.85 us (6%)
  other arithmetic  2 us (2%)
    pallas_call x1, Pallas kernels, reduce_weights(): pl.pallas_call(functools.partial(reduce_kernel, colours, factor), out_sha...  33.7 us
    pallas_call x1, Pallas kernels, body(): pl.pallas_call(functools.partial(post_kernel, n_dom), out_shape=(shape_of...  28.5 us
    pallas_call x1, Pallas kernels, body(): pl.pallas_call(functools.partial(mid_kernel, n_dom), out_shape=(shape_of(...  25.4 us
    pallas_call x1, Pallas kernels, body(): pl.pallas_call(pre_kernel, out_shape=(shape_of(nodes, nodes), shape_of(no...  6.33 us
    unnamed x6, local copies, waits for them, and re-layouts  3.31 us

commit v1 on v0

v1 whole, which is shorter than its diff:
```python
import functools
import math

import jax
import jax.numpy as jnp
import numpy as np
from jax import lax
from jax.experimental import pallas as pl
from jax.experimental.pallas import tpu as pltpu
from jax.sharding import PartitionSpec as P

VMEM = pl.BlockSpec(memory_space=pltpu.VMEM)
SMEM = pl.BlockSpec(memory_space=pltpu.SMEM)
ANY = pl.BlockSpec(memory_space=pl.ANY)
MESH = pl.DeviceIdType.MESH
F32 = jnp.float32
BF16 = jnp.bfloat16


def nn(left, right):
    return lax.dot_general(left, right, (((1,), (0,)), ((), ())), preferred_element_type=F32)


def nt(left, right):
    return lax.dot_general(left, right, (((1,), (1,)), ((), ())), preferred_element_type=F32)


def halves(size):
    return (size // 2, 2) if size % 2 == 0 else (size, 1)


def padded(rows):
    return -(-rows // 16) * 16


def build_kernel(
    outer,
    inner,
    row_ref,
    col_ref,
    keep_ref,
    tile_ref,
    owner_ref,
    rows_ref,
    flag_ref,
    hubs_ref,
    expand_ref,
    lane_ref,
    halo_ref,
    own_ref,
    own_t_ref,
    far_ref,
    far_t_ref,
    gather_ref,
    scatter_ref,
    dense_ref,
    place_ref,
):
    nodes = own_ref.shape[0]
    tiles, block, _ = tile_ref.shape
    own_tiles = nodes // block
    all_tiles = dense_ref.shape[0]
    slots = far_ref.shape[1]
    cap = rows_ref.shape[1]
    groups, hub_per = hubs_ref.shape
    halo_slots = expand_ref.shape[0]
    hub_width = gather_ref.shape[0] - halo_slots
    halo = halo_ref.shape[0]

    dense_ref[...] = jnp.zeros_like(dense_ref)
    for t in range(tiles):

        @pl.when(keep_ref[t] == 1)
        def _():
            rows = pl.ds(pl.multiple_of(row_ref[t] * block, block), block)
            dense_ref[col_ref[t], rows, :] += tile_ref[t].astype(F32)

    place_ref[:halo, :] = halo_ref[...]
    slot = lax.broadcasted_iota(jnp.int32, (hub_per, slots), 1)
    entry = lax.broadcasted_iota(jnp.int32, (hub_per, slots), 0) + halo_slots
    me = lax.axis_index("dom")
    hub = jnp.zeros((1, hub_per), F32)
    for o in range(groups):
        at = halo + o * hub_per
        owner = owner_ref[o]
        seat = lax.rem(owner, inner) * outer + lax.div(owner, inner)
        place_ref[at : at + hub_per, :] = jnp.where(
            slot == entry + seat * hub_width, 1.0, 0.0
        ).astype(BF16)
        owned = (owner == me).astype(F32)
        hub += owned * (hubs_ref[o : o + 1, :].astype(F32) + 1.0)
    far = nn(dense_ref[own_tiles].astype(BF16), place_ref[:block, :])
    for c in range(own_tiles + 1, all_tiles):
        at = (c - own_tiles) * block
        far += nn(dense_ref[c].astype(BF16), place_ref[at : at + block, :])
    far_ref[...] = far.astype(BF16)
    far_t_ref[...] = far.T.astype(BF16)
    for c in range(own_tiles):
        part = dense_ref[c]
        own_ref[:, c * block : (c + 1) * block] = part.astype(BF16)
        own_t_ref[c * block : (c + 1) * block, :] = part.T.astype(BF16)

    chosen = jnp.where(flag_ref[...] == 1, rows_ref[...].astype(F32) + 1.0, 0.0)
    spread = jnp.dot(
        expand_ref[...], chosen, precision=lax.Precision.HIGHEST, preferred_element_type=F32
    )
    from_halo = jnp.where(
        lax.broadcasted_iota(jnp.int32, (halo_slots, cap), 1) == lane_ref[...], spread, 0.0
    )
    from_hub = jnp.where(
        lax.broadcasted_iota(jnp.int32, (hub_width, hub_per), 1)
        == lax.broadcasted_iota(jnp.int32, (hub_width, hub_per), 0),
        jnp.broadcast_to(hub, (hub_width, hub_per)),
        0.0,
    )

    def picked(values):
        pick = (jnp.sum(values, axis=1, keepdims=True) + 0.5).astype(jnp.int32) - 1
        node = lax.broadcasted_iota(jnp.int32, (values.shape[0], nodes), 1)
        return jnp.where(pick == node, 1.0, 0.0)

    halo_pick, hub_pick = picked(from_halo), picked(from_hub)
    gather_ref[:halo_slots, :] = halo_pick.astype(BF16)
    gather_ref[halo_slots:, :] = hub_pick.astype(BF16)
    scatter_ref[...] = (
        jnp.concatenate([halo_pick] + [hub_pick] * outer, axis=0).T.astype(BF16)
    )


def rows_at(start, count):
    return pl.ds(pl.multiple_of(start, 16), count)


class Group:
    def __init__(self, trail, send_sem, recv_sem, sent, landed, where):
        self.send_sem, self.recv_sem = send_sem, recv_sem
        self.sent, self.landed, self.where = sent, landed, where
        trail.append(self)

    def push(self, source, target, where):
        pltpu.make_async_remote_copy(
            src_ref=source,
            dst_ref=target,
            send_sem=self.send_sem,
            recv_sem=self.recv_sem,
            device_id=where,
            device_id_type=MESH,
        ).start()

    def whole(self):
        return pltpu.make_async_remote_copy(
            src_ref=self.sent,
            dst_ref=self.landed,
            send_sem=self.send_sem,
            recv_sem=self.recv_sem,
            device_id=self.where,
            device_id_type=MESH,
        )

    def wait_recv(self):
        self.whole().wait_recv()

    def wait_send(self):
        self.whole().wait_send()


class Segment:
    def __init__(self, place, number, base, rows, refs, trail):
        self.p, self.n, self.base, self.rows, self.trail = place, number, base, rows, trail
        (self.grads, self.core_in, self.kept, self.out, self.inn, self.z_in, self.result) = refs[:7]
        self.send_sem, self.recv_sem = refs[7:]
        p = place
        self.half = rows // p.K
        self.piece = self.half // len(p.square)
        self.half_at = base // p.K
        self.piece_at = base // (p.K * len(p.square))
        self.mine = base + p.k * self.half + p.g * self.piece
        self.small = pl.ds(self.piece_at, self.piece)

    def group(self, stage, sent, landed, where):
        return Group(
            self.trail,
            self.send_sem.at[self.n, stage],
            self.recv_sem.at[self.n, stage],
            sent,
            landed,
            where,
        )

    def core_send(self):
        p = self.p
        if p.K == 1:
            return
        spot = self.core_in.at[pl.ds(self.half_at, self.half)]
        self.core = self.group(0, spot, spot, p.partner)
        give = self.base + p.other_k * self.half
        self.core.push(self.grads.at[rows_at(give, self.half)], spot, p.partner)

    def core_take(self):
        p = self.p
        value = self.grads[rows_at(self.base + p.k * self.half, self.half), :]
        if p.K > 1:
            self.core.wait_recv()
            value = value + self.core_in[pl.ds(self.half_at, self.half), :]
        self.kept[pl.ds(self.half_at, self.half), :] = value
        count = len(p.square)
        for g in range(count):
            self.out[g, self.small, :] = value[g * self.piece : (g + 1) * self.piece].astype(BF16)
        if count > 1:
            some = self.inn.at[pl.ds(0, count - 1), self.small]
            self.square = self.group(1, some, some, p.square_peers[0][1])
            for other, where in p.square_peers:
                self.square.push(
                    self.out.at[other, self.small], self.inn.at[p.g, self.small], where
                )

    def square_take(self):
        p = self.p
        value = self.kept[rows_at(self.half_at + p.g * self.piece, self.piece), :]
        if len(p.square) > 1:
            self.square.wait_recv()
            for other, _ in p.square_peers:
                value = value + self.inn[other, self.small, :].astype(F32)
        self.z_in[p.z, self.small, :] = value.astype(BF16)
        if p.Z > 1:
            some = self.z_in.at[pl.ds(0, p.Z - 1), self.small]
            self.line = self.group(2, some, some, p.z_peers[0][1])
            spot = self.z_in.at[p.z, self.small]
            for _, where in p.z_peers:
                self.line.push(spot, spot, where)

    def line_take(self, factor):
        p = self.p
        if p.Z > 1:
            self.line.wait_recv()
        value = self.z_in[0, self.small, :].astype(F32)
        for i in range(1, p.Z):
            value = value + self.z_in[i, self.small, :].astype(F32)
        spot = rows_at(self.mine, self.piece)
        self.result[spot, :] = (value * factor).astype(BF16)
        count = len(p.square)
        if count > 1:
            some = self.result.at[pl.ds(self.base, (count - 1) * self.piece)]
            self.spread = self.group(3, some, some, p.square_peers[0][1])
            for _, where in p.square_peers:
                self.spread.push(self.result.at[spot], self.result.at[spot], where)

    def spread_take(self):
        p = self.p
        if len(p.square) > 1:
            self.spread.wait_recv()
        if p.K > 1:
            spot = self.result.at[rows_at(self.base + p.k * self.half, self.half)]
            self.last = self.group(4, spot, spot, p.partner)
            self.last.push(spot, spot, p.partner)

    def finish(self):
        if self.p.K > 1:
            self.last.wait_recv()


class Place:
    def __init__(self, n_dom, n_batch):
        self.D = n_dom
        self.Z, self.Y = halves(n_dom)
        self.X, self.K = halves(n_batch)
        self.me = lax.axis_index("dom")
        batch = lax.axis_index("batch")
        self.z, self.y = lax.div(self.me, self.Y), lax.rem(self.me, self.Y)
        self.x, self.k = lax.div(batch, self.K), lax.rem(batch, self.K)
        self.other_k = lax.rem(self.k + 1, self.K)
        self.partner = {"batch": self.x * self.K + self.other_k}
        self.dom_peers = [lax.rem(self.me + d, n_dom) for d in range(1, n_dom)]
        self.z_peers = []
        for d in range(1, self.Z):
            seat = lax.rem(self.z + d, self.Z)
            self.z_peers.append((seat, {"dom": seat * self.Y + self.y}))
        self.y_peers = []
        for d in range(1, self.Y):
            seat = lax.rem(self.y + d, self.Y)
            self.y_peers.append((seat, {"dom": self.z * self.Y + seat}))
        self.square = range(self.X * self.Y)
        self.g = self.x * self.Y + self.y
        self.square_peers = []
        for d in range(1, self.X * self.Y):
            seat = lax.rem(self.g + d, self.X * self.Y)
            where = {
                "batch": lax.div(seat, self.Y) * self.K + self.k,
                "dom": self.z * self.Y + lax.rem(seat, self.Y),
            }
            self.square_peers.append((seat, where))

    def greet(self):
        barrier = pltpu.get_barrier_semaphore()
        peers = [{"dom": other} for other in self.dom_peers]
        if self.K > 1:
            peers.append(self.partner)
        for x in range(1, self.X):
            for y in range(self.Y):
                peers.append(
                    {
                        "batch": lax.rem(self.x + x, self.X) * self.K + self.k,
                        "dom": self.z * self.Y + lax.rem(self.y + y, self.Y),
                    }
                )
        for where in peers:
            pl.semaphore_signal(barrier, inc=1, device_id=where, device_id_type=MESH)
        return lambda: pl.semaphore_wait(barrier, len(peers))


def main_kernel(
    n_dom,
    n_batch,
    hub_w,
    factor,
    sig_ref,
    cot_ref,
    conv_ref,
    mix_ref,
    own_ref,
    own_t_ref,
    far_ref,
    far_t_ref,
    gather_ref,
    scatter_ref,
    layer_ref,
    sgrad_ref,
    result_ref,
    wide_ref,
    wide_t_ref,
    cot_t_ref,
    taps_ref,
    hidden_ref,
    hop_ref,
    back_ref,
    back_one_ref,
    slope_filt,
    slope_gate,
    hop_sum,
    back_sum,
    held_ref,
    sgrad_wide,
    grads_ref,
    out_b,
    hub_b,
    hub_in,
    hub_out,
    in_b,
    out_f,
    in_f,
    core_in,
    kept,
    square_out,
    square_in,
    z_in,
    halo_send,
    halo_recv,
    hub_send,
    hub_recv,
    seg_send,
    seg_recv,
):
    steps, nodes, chans = cot_ref.shape
    p = Place(n_dom, n_batch)
    D, Z, Y = p.D, p.Z, p.Y
    ready = p.greet()
    halo = gather_ref.shape[0] - hub_w
    hw = halo // D
    trail = []
    span = [slice(t * chans, (t + 1) * chans) for t in range(steps + 1)]
    pair = [slice(t * chans, (t + 2) * chans) for t in range(steps)]

    def group(sems, e, kind, t, sent, landed, where):
        return Group(
            trail, sems[0].at[e, kind, t], sems[1].at[e, kind, t], sent, landed, where
        )

    halo_sems, hub_sems = (halo_send, halo_recv), (hub_send, hub_recv)
    groups = {}

    def send_halo(e, kind, t):
        out, inn = (out_b, in_b) if kind == 0 else (out_f, in_f)
        some = inn.at[e, t, pl.ds(0, (D - 1) * hw)]
        g = group(halo_sems, e, kind, t, some, some, {"dom": p.dom_peers[0]})
        mine = rows_at(p.me * hw, hw)
        for other in p.dom_peers:
            g.push(
                out.at[e, t, rows_at(other * hw, hw)], inn.at[e, t, mine], {"dom": other}
            )
        groups["halo", e, kind, t] = g
        inn[e, t, mine, :] = out[e, t, mine, :]

    def send_hub_b(e, t):
        if Y == 1:
            return
        g = group(hub_sems, e, 0, t, hub_in.at[e, t], hub_in.at[e, t], p.y_peers[0][1])
        for seat, where in p.y_peers:
            g.push(
                out_b.at[e, t, rows_at(halo + seat * (Z * hub_w), Z * hub_w)],
                hub_in.at[e, t],
                where,
            )
        groups["hub", e, 0, t] = g

    def turn_hub_b(e, t):
        value = hub_b[e, t, rows_at(p.y * (Z * hub_w), Z * hub_w), :]
        if Y > 1:
            groups["hub", e, 0, t].wait_recv()
            value = value + hub_in[e, t].astype(F32)
        hub_out[e, t] = value.astype(BF16)
        mine = rows_at(halo + p.z * hub_w, hub_w)
        if Z > 1:
            some = in_b.at[e, t, pl.ds(halo, (Z - 1) * hub_w)]
            g = group(hub_sems, e, 1, t, some, some, p.z_peers[0][1])
            for seat, where in p.z_peers:
                g.push(hub_out.at[e, t, rows_at(seat * hub_w, hub_w)], in_b.at[e, t, mine], where)
            groups["hub", e, 1, t] = g
        in_b[e, t, mine, :] = hub_out[e, t, rows_at(p.z * hub_w, hub_w), :]

    def take_b(e, t):
        if D > 1:
            groups["halo", e, 0, t].wait_recv()
        if Z > 1:
            groups["hub", e, 1, t].wait_recv()
        return nn(scatter_ref[...], in_b[e, t])

    def send_hub_f(e, t):
        mine = rows_at(halo + (p.y * Z + p.z) * hub_w, hub_w)
        if Z > 1:
            some = in_f.at[e, t, pl.ds(halo, (Z - 1) * hub_w)]
            g = group(hub_sems, e, 2, t, some, some, p.z_peers[0][1])
            for _, where in p.z_peers:
                g.push(out_f.at[e, t, pl.ds(halo, hub_w)], in_f.at[e, t, mine], where)
            groups["hub", e, 2, t] = g
        in_f[e, t, mine, :] = out_f[e, t, halo:, :]

    def turn_hub_f(e, t):
        if Z > 1:
            groups["hub", e, 2, t].wait_recv()
        if Y > 1:
            column = in_f.at[e, t, rows_at(halo + p.y * (Z * hub_w), Z * hub_w)]
            g = group(hub_sems, e, 3, t, column, column, p.y_peers[0][1])
            for _, where in p.y_peers:
                g.push(column, column, where)
            groups["hub", e, 3, t] = g

    def take_f(e, t):
        if D > 1:
            groups["halo", e, 1, t].wait_recv()
        if Y > 1:
            groups["hub", e, 3, t].wait_recv()
        return nn(far_ref[...], in_f[e, t])

    def put_b(e, t, field):
        value = nn(far_t_ref[...], field)
        out_b[e, t] = value.astype(BF16)
        hub_b[e, t] = value[halo:]

    def segment(number, base, rows):
        refs = (
            grads_ref,
            core_in,
            kept,
            square_out,
            square_in,
            z_in,
            result_ref,
            seg_send,
            seg_recv,
        )
        return Segment(p, number, base * chans, rows * chans, refs, trail)

    filt_seg, gate_seg, mix_seg, last_seg = (
        segment(0, 0, 2),
        segment(1, 2, 2),
        segment(2, 4, 2),
        segment(3, 6, 1),
    )

    for t in range(steps):
        back = nt(cot_ref[t], mix_ref[2]).astype(BF16)
        back_ref[t] = back
        put_b(0, t, back)
    ready()
    for t in range(steps):
        send_hub_b(0, t)
    for t in range(steps):
        send_halo(0, 0, t)

    wide_ref[...] = sig_ref[...].reshape(nodes, (steps + 1) * chans)
    for kind in range(2):
        for tap in range(2):
            taps_ref[span[tap], span[kind]] = conv_ref[kind, tap]
    edge = nn(gather_ref[...], wide_ref[...]).astype(BF16)
    for t in range(steps):
        both = nn(edge[:, pair[t]], taps_ref[...])
        out_f[0, t] = (jnp.tanh(both[:, :chans]) * jax.nn.sigmoid(both[:, chans:])).astype(BF16)
    for t in range(steps):
        turn_hub_b(0, t)
    for t in range(steps):
        send_hub_f(0, t)
    for t in range(steps):
        send_halo(0, 1, t)

    for t in range(steps):
        back_sum[t] = nt(cot_ref[t], mix_ref[1]) + nn(own_t_ref[...], back_ref[t])
    for t in range(steps):
        both = nn(wide_ref[:, pair[t]], taps_ref[...])
        tanh_filt = jnp.tanh(both[:, :chans])
        sig_gate = jax.nn.sigmoid(both[:, chans:])
        hidden_ref[t] = (tanh_filt * sig_gate).astype(BF16)
        slope_filt[t] = sig_gate * (1.0 - tanh_filt * tanh_filt)
        slope_gate[t] = tanh_filt * sig_gate * (1.0 - sig_gate)
    for t in range(steps):
        turn_hub_f(0, t)

    for t in range(steps):
        back = (back_sum[t] + take_b(0, t)).astype(BF16)
        back_one_ref[t] = back
        put_b(1, t, back)
        send_hub_b(1, t)
        send_halo(1, 0, t)
    for t in range(steps):
        hop_sum[t] = nn(own_ref[...], hidden_ref[t])
    for t in range(steps):
        turn_hub_b(1, t)

    for t in range(steps):
        hop = (hop_sum[t] + take_f(0, t)).astype(BF16)
        hop_ref[t] = hop
        out_f[1, t] = nn(gather_ref[...], hop).astype(BF16)
        send_hub_f(1, t)
        send_halo(1, 1, t)

    wide_t_ref[...] = wide_ref[...].T
    for t in range(steps):
        back_sum[t] = nt(cot_ref[t], mix_ref[0]) + nn(own_t_ref[...], back_one_ref[t])
    for t in range(steps):
        turn_hub_f(1, t)

    for t in range(steps):
        grad_hidden = back_sum[t] + take_b(1, t)
        held_ref[t, :, :chans] = (grad_hidden * slope_filt[t]).astype(BF16)
        held_ref[t, :, chans:] = (grad_hidden * slope_gate[t]).astype(BF16)
    for kind, seg in enumerate((filt_seg, gate_seg)):
        outer = nn(wide_t_ref[pair[0], :], held_ref[0, :, span[kind]])
        for t in range(1, steps):
            outer += nn(wide_t_ref[pair[t], :], held_ref[t, :, span[kind]])
        grads_ref[kind * 2 * chans : (kind + 1) * 2 * chans, :] = outer
        seg.core_send()
    for t in range(steps):
        cot_t_ref[t] = cot_ref[t].T
    for spot, field in enumerate((hidden_ref, hop_ref)):
        part = nn(cot_t_ref[0], field[0])
        for t in range(1, steps):
            part += nn(cot_t_ref[t], field[t])
        grads_ref[(4 + spot) * chans : (5 + spot) * chans, :] = part.T
    filt_seg.core_take()
    gate_seg.core_take()
    mix_seg.core_send()

    for t in range(steps):
        hop_sum[t] = nn(own_ref[...], hop_ref[t])
    mix_seg.core_take()
    part = None
    for t in range(steps):
        hop = (hop_sum[t] + take_f(1, t)).astype(BF16)
        hop_sum[t] = nn(hop, mix_ref[2])
        here = nn(cot_t_ref[t], hop)
        part = here if part is None else part + here
    grads_ref[6 * chans :, :] = part.T
    last_seg.core_send()
    filt_seg.square_take()
    gate_seg.square_take()
    last_seg.core_take()
    mix_seg.square_take()
    for t in range(steps):
        layer_ref[t] = (
            wide_ref[:, span[t + 1]].astype(F32)
            + nn(hidden_ref[t], mix_ref[0])
            + nn(hop_ref[t], mix_ref[1])
            + hop_sum[t]
        ).astype(BF16)
    last_seg.square_take()
    carried = None
    for t in range(steps):
        into = nt(held_ref[t], taps_ref[...])
        before = into[:, :chans]
        if t > 0:
            before = before + carried
        sgrad_wide[:, span[t]] = before.astype(BF16)
        carried = into[:, chans:] + cot_ref[t].astype(F32)
    sgrad_wide[:, span[steps]] = carried.astype(BF16)
    sgrad_ref[...] = sgrad_wide[...].reshape(sgrad_ref.shape)
    order = (filt_seg, gate_seg, mix_seg, last_seg)
    for seg in order:
        seg.line_take(factor)
    for seg in order:
        seg.spread_take()
    for seg in order:
        seg.finish()
    for g in trail:
        g.wait_send()


def finish_kernel(layer_ref, sgrad_ref, result_ref, layer_out, sgrad_out, conv_out, mix_out, sems):
    copies = [
        pltpu.make_async_copy(layer_ref, layer_out, sems.at[0]),
        pltpu.make_async_copy(sgrad_ref, sgrad_out, sems.at[1]),
    ]
    for copy in copies:
        copy.start()
    rows = conv_out.shape[0]
    conv_out[...] = result_ref[:rows, :].astype(F32)
    mix_out[...] = result_ref[rows:, :].astype(F32)
    for copy in copies:
        copy.wait()


def shape_of(*dims, dtype=BF16):
    return jax.ShapeDtypeStruct(dims, dtype)


def body(
    axis_sizes,
    signal,
    cotangent,
    conv_weight,
    mix_weight,
    send_rows,
    send_mask,
    tile_vals,
    tile_row,
    tile_col,
    tile_mask,
    hub_owner,
    hub_rows,
):
    nodes, b_dev, hist, chans = signal.shape
    steps = hist - 1
    n_dom, cap = send_rows.shape
    n_batch = dict(axis_sizes)["batch"]
    outer, inner = halves(n_dom)
    square = halves(n_batch)[0] * inner
    pair = halves(n_batch)[1]
    hub_per = hub_rows.shape[1]
    hw, hub_w = padded(cap), padded(hub_per)
    halo = n_dom * hw
    slots = halo + n_dom * hub_w
    back_rows = halo + outer * hub_w
    lead_rows = halo + hub_w
    block = tile_vals.shape[1]
    entries = n_dom * cap + hub_rows.size
    all_tiles = (nodes + entries) // block

    sig = signal.reshape(nodes, hist, chans)
    cot = jnp.transpose(cotangent.reshape(nodes, steps, chans), (1, 0, 2))

    slot = np.arange(halo)
    expand = (slot[:, None] // hw == np.arange(n_dom)[None, :]).astype(np.float32)
    lane = (slot % hw).astype(np.int32)[:, None]
    entry = np.arange(n_dom * cap)
    halo_place = jnp.asarray(
        (entry // cap * hw + entry % cap)[:, None] == np.arange(slots)[None, :], dtype=BF16
    )

    mats = pl.pallas_call(
        functools.partial(build_kernel, outer, inner),
        out_shape=(
            shape_of(nodes, nodes),
            shape_of(nodes, nodes),
            shape_of(nodes, slots),
            shape_of(slots, nodes),
            shape_of(lead_rows, nodes),
            shape_of(nodes, back_rows),
        ),
        in_specs=[SMEM] * 3 + [VMEM] + [SMEM] + [VMEM] * 6,
        out_specs=(VMEM,) * 6,
        scratch_shapes=[
            pltpu.VMEM((all_tiles, nodes, block), F32),
            pltpu.VMEM((entries, slots), BF16),
        ],
        name="build",
    )(
        tile_row,
        tile_col,
        tile_mask,
        tile_vals,
        hub_owner,
        send_rows,
        send_mask,
        hub_rows,
        expand,
        lane,
        halo_place,
    )

    total_count = nodes * steps * b_dev
    for _, size in axis_sizes:
        total_count *= size
    weights = 7 * chans
    field = pltpu.VMEM((steps, nodes, chans), BF16)
    total = pltpu.VMEM((steps, nodes, chans), F32)
    wide = pltpu.VMEM((nodes, hist * chans), BF16)
    halo_sems = pltpu.SemaphoreType.DMA((2, 2, steps))
    hub_sems = pltpu.SemaphoreType.DMA((2, 4, steps))
    seg_sems = pltpu.SemaphoreType.DMA((4, 5))
    layer, sgrad, result = pl.pallas_call(
        functools.partial(
            main_kernel, n_dom, n_batch, hub_w, 1.0 / math.sqrt(total_count)
        ),
        out_shape=(
            shape_of(steps, nodes, chans),
            shape_of(nodes, hist, chans),
            shape_of(weights, chans),
        ),
        in_specs=[VMEM] * 10,
        out_specs=(VMEM,) * 3,
        scratch_shapes=[
            wide,
            pltpu.VMEM((hist * chans, nodes), BF16),
            pltpu.VMEM((steps, chans, nodes), BF16),
            pltpu.VMEM((2 * chans, 2 * chans), BF16),
            field,
            field,
            field,
            field,
            total,
            total,
            total,
            total,
            pltpu.VMEM((steps, nodes, 2 * chans), BF16),
            wide,
            pltpu.VMEM((weights, chans), F32),
            pltpu.VMEM((2, steps, slots, chans), BF16),
            pltpu.VMEM((2, steps, n_dom * hub_w, chans), F32),
            pltpu.VMEM((2, steps, outer * hub_w, chans), BF16),
            pltpu.VMEM((2, steps, outer * hub_w, chans), BF16),
            pltpu.VMEM((2, steps, back_rows, chans), BF16),
            pltpu.VMEM((2, steps, lead_rows, chans), BF16),
            pltpu.VMEM((2, steps, slots, chans), BF16),
            pltpu.VMEM((weights // pair, chans), F32),
            pltpu.VMEM((weights // pair, chans), F32),
            pltpu.VMEM((square, weights // (pair * square), chans), BF16),
            pltpu.VMEM((square, weights // (pair * square), chans), BF16),
            pltpu.VMEM((outer, weights // (pair * square), chans), BF16),
            halo_sems,
            halo_sems,
            hub_sems,
            hub_sems,
            seg_sems,
            seg_sems,
        ],
        compiler_params=pltpu.CompilerParams(collective_id=0, has_side_effects=True),
        name="main",
    )(sig, cot, conv_weight, mix_weight, *mats)

    layer_out, signal_grad, conv_grad, mix_grad = pl.pallas_call(
        finish_kernel,
        out_shape=(
            shape_of(steps, nodes, chans),
            shape_of(nodes, hist, chans),
            shape_of(4 * chans, chans, dtype=F32),
            shape_of(3 * chans, chans, dtype=F32),
        ),
        in_specs=[VMEM] * 3,
        out_specs=(ANY, ANY, VMEM, VMEM),
        scratch_shapes=[pltpu.SemaphoreType.DMA((2,))],
        name="finish",
    )(layer, sgrad, result)
    return (
        jnp.transpose(layer_out, (1, 0, 2)).reshape(nodes, b_dev, steps, chans),
        signal_grad.reshape(signal.shape),
        conv_grad.reshape(conv_weight.shape),
        mix_grad.reshape(mix_weight.shape),
    )


def solution(mesh):
    placed = (
        P("dom", "batch", None, None),
        P("dom", "batch", None, None),
        P(),
        P(),
        P("dom", None),
        P("dom", None),
        P("dom", None, None),
        P("dom"),
        P("dom"),
        P("dom"),
        P(),
        P(),
    )
    axis_sizes = tuple((axis, mesh.shape[axis]) for axis in ("dom", "batch"))
    return jax.shard_map(
        functools.partial(body, axis_sizes),
        mesh=mesh,
        in_specs=placed,
        out_specs=(P("dom", "batch", None, None), P("dom", "batch", None, None), P(), P()),
        check_vma=False,
    )
```

time: 103 us -> 67.7 us (0.66)
  Pallas kernels: 93.9 us -> 66.9 us
  local copies, waits for them, and re-layouts: 5.85 us -> 0 us
  other arithmetic: 2 us -> 0 us
    pallas_call x4 -> x3, Pallas kernels: 93.9 us -> 66.9 us  [the longest x1 59.8 us: body(): pl.pallas_call(functools.partial(main_kernel, n_dom, n_batch, hub_w, 1.0...]
    unnamed x6 -> x0, local copies, waits for them, and re-layouts: 3.31 us -> none
    reshape x2 -> x0, other arithmetic: 2 us -> none  [the longest x1 1.06 us: body(): reduced[:4 * chans].astype(F32).reshape(conv_weight.shape)]
    reshape x1 -> x0, local copies, waits for them, and re-layouts: 1.56 us -> none  [body(): signal_grad.reshape(signal.shape)]
where the time goes in v1:
time: 67.7 us; the launch traced here: 67.5 us
  Pallas kernels  66.9 us (99%)
    pallas_call x1, Pallas kernels, body(): pl.pallas_call(functools.partial(main_kernel, n_dom, n_batch, hub_w, 1.0...  59.8 us
    pallas_call x1, Pallas kernels, body(): pl.pallas_call(finish_kernel, out_shape=(shape_of(steps, nodes, chans), s...  4.2 us
    pallas_call x1, Pallas kernels, body(): pl.pallas_call(functools.partial(build_kernel, outer, inner), out_shape=(...  2.93 us

profile of v1, /device:TPU:0, one launch (start us, length us, event | category | flops | bytes accessed | tf_op | source)
XLA Modules:
  0.0 67.5 jit_solution(7047812098815715830)
XLA Ops:
  0.6 2.9 %build.1 = (bf16[512,512]{1,0:T(8,128)(2,1)}, bf16[512,512]{1,0:T(8,128)(2,1)}, bf16[512,256]{1,0:T(8,128)(2,1)}, bf16[256,512]{1,0:T(8,128)(2,1)}, bf16[144,512]{1,0:T(8,128)(2,1)}, /*index=5*/bf16[512,192]{1,0:T(8,128)(2,1)}) custom-call(s32[16]{0:T(128)} %row_ref.1, s32[16]{0:T(128)} %col_ref.1, s32[16]{0:T(128)} %keep_ref.1, ...), custom_call_target="tpu_custom_call" | custom-call | tf_op jit(solution)/shard_map/build/pallas_call | solution.py:667
  3.6 59.8 %main.1 = (bf16[3,512,256]{2,1,0:T(8,128)(2,1)}, bf16[512,4,256]{2,1,0:T(4,128)(2,1)}, bf16[1792,256]{1,0:T(8,128)(2,1)}) custom-call(bf16[512,4,256]{2,1,0:T(4,128)(2,1)} %bitcast.12, bf16[3,512,256]{2,1,0:T(8,128)(2,1)} %bitcast.13, bf16[2,2,256,256]{3,2,1,0:T(8,128)(2,1)} %conv_ref.1, bf16[3,256,256]{2,1,0:T(8,128)(2,1)} %mix_ref.1, ...), custom_call_target="tpu_custom_call" | custom-call | tf_op jit(solution)/shard_map/main/pallas_call | solution.py:708
  63.3 4.2 %finish.1 = (bf16[3,512,256]{2,1,0:T(8,128)(2,1)}, bf16[512,4,256]{2,1,0:T(4,128)(2,1)}, f32[1024,256]{1,0:T(8,128)}, f32[768,256]{1,0:T(8,128)}) custom-call(bf16[3,512,256]{2,1,0:T(8,128)(2,1)} %get-tuple-element.23.layer_ref, bf16[512,4,256]{2,1,0:T(4,128)(2,1)} %get-tuple-element.24.sgrad_ref, bf16[1792,256]{1,0:T(8,128)(2,1)} %get-tuple-element.25.result_ref), custom_call_target="tpu_custom_call" | custom-call | tf_op jit(solution)/shard_map/finish/pallas_call | solution.py:758

commit v2 on v1

--- a/solution.py
+++ b/solution.py
@@ -3,16 +3,16 @@
 
 import jax
 import jax.numpy as jnp
-import numpy as np
 from jax import lax
 from jax.experimental import pallas as pl
 from jax.experimental.pallas import tpu as pltpu
 from jax.sharding import PartitionSpec as P
 
 VMEM = pl.BlockSpec(memory_space=pltpu.VMEM)
-SMEM = pl.BlockSpec(memory_space=pltpu.SMEM)
 ANY = pl.BlockSpec(memory_space=pl.ANY)
+HBM = pl.BlockSpec(memory_space=pltpu.HBM)
 MESH = pl.DeviceIdType.MESH
+BUILD_ROOM = 52 << 20
 F32 = jnp.float32
 BF16 = jnp.bfloat16
 
@@ -27,6 +27,14 @@
 
 def halves(size):
     return (size // 2, 2) if size % 2 == 0 else (size, 1)
+
+
+def flipped(index, size):
+    total, low, high = 0, 1, size // 2
+    while high >= 1:
+        total = total + lax.rem(lax.div(index, low), 2) * high
+        low, high = low * 2, high // 2
+    return total
 
 
 def padded(rows):
@@ -36,17 +44,12 @@
 def build_kernel(
     outer,
     inner,
-    row_ref,
-    col_ref,
-    keep_ref,
-    tile_ref,
-    owner_ref,
-    rows_ref,
-    flag_ref,
-    hubs_ref,
-    expand_ref,
-    lane_ref,
-    halo_ref,
+    n_dom,
+    hub_width,
+    cap,
+    hub_per,
+    table_any,
+    tile_any,
     own_ref,
     own_t_ref,
     far_ref,
@@ -55,40 +58,67 @@
     scatter_ref,
     dense_ref,
     place_ref,
+    ints_ref,
+    table_ref,
+    tile_ref,
+    sems,
 ):
+    loads = [
+        pltpu.make_async_copy(source, target, sems.at[i])
+        for i, (source, target) in enumerate(
+            (
+                (table_any, ints_ref),
+                (table_any, table_ref),
+                (tile_any, tile_ref),
+            )
+        )
+    ]
+    for load in loads:
+        load.start()
     nodes = own_ref.shape[0]
     tiles, block, _ = tile_ref.shape
     own_tiles = nodes // block
     all_tiles = dense_ref.shape[0]
     slots = far_ref.shape[1]
-    cap = rows_ref.shape[1]
-    groups, hub_per = hubs_ref.shape
-    halo_slots = expand_ref.shape[0]
-    hub_width = gather_ref.shape[0] - halo_slots
-    halo = halo_ref.shape[0]
+    groups = ints_ref.shape[0] - 4 - 2 * n_dom
+    rows_ref, flag_ref = table_ref.at[4 : 4 + n_dom], table_ref.at[4 + n_dom : 4 + 2 * n_dom]
+    hubs_ref = table_ref.at[4 + 2 * n_dom :]
+    halo_slots = gather_ref.shape[0] - hub_width
+    halo_width = halo_slots // n_dom
+    halo = n_dom * cap
 
     dense_ref[...] = jnp.zeros_like(dense_ref)
+    entry = lax.broadcasted_iota(jnp.int32, (halo, slots), 0)
+    if cap != halo_width:
+        entry = lax.div(entry, cap) * halo_width + lax.rem(entry, cap)
+    place_ref[:halo, :] = jnp.where(
+        entry == lax.broadcasted_iota(jnp.int32, (halo, slots), 1), 1.0, 0.0
+    ).astype(BF16)
+    source = lax.div(lax.broadcasted_iota(jnp.int32, (halo_slots, n_dom), 0), halo_width)
+    expand = (source == lax.broadcasted_iota(jnp.int32, (halo_slots, n_dom), 1)).astype(F32)
+    lane = lax.rem(lax.broadcasted_iota(jnp.int32, (halo_slots, cap), 0), halo_width)
+    for load in loads:
+        load.wait()
     for t in range(tiles):
 
-        @pl.when(keep_ref[t] == 1)
+        @pl.when(ints_ref[2, t] == 1)
         def _():
-            rows = pl.ds(pl.multiple_of(row_ref[t] * block, block), block)
-            dense_ref[col_ref[t], rows, :] += tile_ref[t].astype(F32)
-
-    place_ref[:halo, :] = halo_ref[...]
+            rows = pl.ds(pl.multiple_of(ints_ref[0, t] * block, block), block)
+            dense_ref[ints_ref[1, t], rows, :] += tile_ref[t].astype(F32)
+
     slot = lax.broadcasted_iota(jnp.int32, (hub_per, slots), 1)
     entry = lax.broadcasted_iota(jnp.int32, (hub_per, slots), 0) + halo_slots
     me = lax.axis_index("dom")
     hub = jnp.zeros((1, hub_per), F32)
     for o in range(groups):
         at = halo + o * hub_per
-        owner = owner_ref[o]
-        seat = lax.rem(owner, inner) * outer + lax.div(owner, inner)
+        owner = ints_ref[3, o]
+        seat = lax.rem(owner, inner) * outer + flipped(lax.div(owner, inner), outer)
         place_ref[at : at + hub_per, :] = jnp.where(
             slot == entry + seat * hub_width, 1.0, 0.0
         ).astype(BF16)
         owned = (owner == me).astype(F32)
-        hub += owned * (hubs_ref[o : o + 1, :].astype(F32) + 1.0)
+        hub += owned * (hubs_ref[o : o + 1, :hub_per].astype(F32) + 1.0)
     far = nn(dense_ref[own_tiles].astype(BF16), place_ref[:block, :])
     for c in range(own_tiles + 1, all_tiles):
         at = (c - own_tiles) * block
@@ -100,12 +130,12 @@
         own_ref[:, c * block : (c + 1) * block] = part.astype(BF16)
         own_t_ref[c * block : (c + 1) * block, :] = part.T.astype(BF16)
 
-    chosen = jnp.where(flag_ref[...] == 1, rows_ref[...].astype(F32) + 1.0, 0.0)
+    chosen = jnp.where(flag_ref[:, :cap] == 1, rows_ref[:, :cap].astype(F32) + 1.0, 0.0)
     spread = jnp.dot(
-        expand_ref[...], chosen, precision=lax.Precision.HIGHEST, preferred_element_type=F32
+        expand, chosen, precision=lax.Precision.HIGHEST, preferred_element_type=F32
     )
     from_halo = jnp.where(
-        lax.broadcasted_iota(jnp.int32, (halo_slots, cap), 1) == lane_ref[...], spread, 0.0
+        lax.broadcasted_iota(jnp.int32, (halo_slots, cap), 1) == lane, spread, 0.0
     )
     from_hub = jnp.where(
         lax.broadcasted_iota(jnp.int32, (hub_width, hub_per), 1)
@@ -123,7 +153,7 @@
     gather_ref[:halo_slots, :] = halo_pick.astype(BF16)
     gather_ref[halo_slots:, :] = hub_pick.astype(BF16)
     scatter_ref[...] = (
-        jnp.concatenate([halo_pick] + [hub_pick] * outer, axis=0).T.astype(BF16)
+        jnp.concatenate([halo_pick] + [hub_pick] * min(outer, 2), axis=0).T.astype(BF16)
     )
 
 
@@ -279,6 +309,16 @@
         for d in range(1, self.Y):
             seat = lax.rem(self.y + d, self.Y)
             self.y_peers.append((seat, {"dom": self.z * self.Y + seat}))
+        assert self.Z & (self.Z - 1) == 0
+        self.seat = flipped(self.z, self.Z)
+        self.depth = self.Z.bit_length() - 1
+        self.z_pairs = []
+        for i in range(self.depth):
+            stride = self.Z >> (i + 1)
+            other = self.z + stride - 2 * stride * lax.rem(lax.div(self.z, stride), 2)
+            kept = self.seat - lax.rem(self.seat, 1 << i)
+            given = kept + (1 << i) - 2 * (1 << i) * lax.rem(lax.div(kept, 1 << i), 2)
+            self.z_pairs.append((kept, given, {"dom": other * self.Y + self.y}))
         self.square = range(self.X * self.Y)
         self.g = self.x * self.Y + self.y
         self.square_peers = []
@@ -344,6 +384,8 @@
     out_b,
     hub_b,
     hub_in,
+    hub_sum,
+    hub_land,
     hub_out,
     in_b,
     out_f,
@@ -402,20 +444,39 @@
             )
         groups["hub", e, 0, t] = g
 
-    def turn_hub_b(e, t):
-        value = hub_b[e, t, rows_at(p.y * (Z * hub_w), Z * hub_w), :]
-        if Y > 1:
-            groups["hub", e, 0, t].wait_recv()
-            value = value + hub_in[e, t].astype(F32)
-        hub_out[e, t] = value.astype(BF16)
-        mine = rows_at(halo + p.z * hub_w, hub_w)
-        if Z > 1:
-            some = in_b.at[e, t, pl.ds(halo, (Z - 1) * hub_w)]
-            g = group(hub_sems, e, 1, t, some, some, p.z_peers[0][1])
-            for seat, where in p.z_peers:
-                g.push(hub_out.at[e, t, rows_at(seat * hub_w, hub_w)], in_b.at[e, t, mine], where)
-            groups["hub", e, 1, t] = g
-        in_b[e, t, mine, :] = hub_out[e, t, rows_at(p.z * hub_w, hub_w), :]
+    def pair_b(e, t, i):
+        kept, given, where = p.z_pairs[i]
+        count = hub_w << i
+        spot = rows_at(given * hub_w, count)
+        hub_out[e, t, spot, :] = hub_sum[e, t, spot, :].astype(BF16)
+        if i == 0:
+            land = in_b.at[e, t, pl.ds(halo + hub_w, hub_w)]
+        else:
+            land = hub_land.at[e, t, pl.ds(count, count)]
+        g = group(hub_sems, e, 1 + i, t, land, land, where)
+        g.push(hub_out.at[e, t, spot], land, where)
+        groups["hub", e, 1 + i, t] = g
+
+    def turn_b(e, t, j):
+        if j == 0:
+            value = hub_b[t, rows_at(p.y * (Z * hub_w), Z * hub_w), :]
+            if Y > 1:
+                groups["hub", e, 0, t].wait_recv()
+                value = value + hub_in[e, t].astype(F32)
+            hub_sum[e, t] = value
+        else:
+            i = p.depth - j
+            kept, count = p.z_pairs[i][0], hub_w << i
+            groups["hub", e, 1 + i, t].wait_recv()
+            hub_sum[e, t, rows_at(kept * hub_w, count), :] += hub_land[
+                e, t, pl.ds(count, count), :
+            ].astype(F32)
+        if j < p.depth:
+            pair_b(e, t, p.depth - 1 - j)
+        if j == max(p.depth - 1, 0):
+            in_b[e, t, pl.ds(halo, hub_w), :] = hub_sum[
+                e, t, rows_at(p.seat * hub_w, hub_w), :
+            ].astype(BF16)
 
     def take_b(e, t):
         if D > 1:
@@ -424,37 +485,62 @@
             groups["hub", e, 1, t].wait_recv()
         return nn(scatter_ref[...], in_b[e, t])
 
+    def pair_f(e, t, i):
+        kept, given, where = p.z_pairs[i]
+        base, count = halo + p.y * (Z * hub_w), hub_w << i
+        land = in_f.at[e, t, rows_at(base + given * hub_w, count)]
+        spot = in_f.at[e, t, rows_at(base + kept * hub_w, count)]
+        source = out_f.at[e, t, pl.ds(halo, hub_w)] if i == 0 else spot
+        g = group(hub_sems, e, 1 + p.depth + i, t, land, land, where)
+        g.push(source, spot, where)
+        groups["row", e, i, t] = g
+
+    def column_f(e, t):
+        if Y == 1:
+            return
+        column = in_f.at[e, t, rows_at(halo + p.y * (Z * hub_w), Z * hub_w)]
+        g = group(hub_sems, e, 1 + 2 * p.depth, t, column, column, p.y_peers[0][1])
+        for _, where in p.y_peers:
+            g.push(column, column, where)
+        groups["row", e, p.depth, t] = g
+
     def send_hub_f(e, t):
-        mine = rows_at(halo + (p.y * Z + p.z) * hub_w, hub_w)
-        if Z > 1:
-            some = in_f.at[e, t, pl.ds(halo, (Z - 1) * hub_w)]
-            g = group(hub_sems, e, 2, t, some, some, p.z_peers[0][1])
-            for _, where in p.z_peers:
-                g.push(out_f.at[e, t, pl.ds(halo, hub_w)], in_f.at[e, t, mine], where)
-            groups["hub", e, 2, t] = g
+        mine = rows_at(halo + (p.y * Z + p.seat) * hub_w, hub_w)
         in_f[e, t, mine, :] = out_f[e, t, halo:, :]
-
-    def turn_hub_f(e, t):
-        if Z > 1:
-            groups["hub", e, 2, t].wait_recv()
-        if Y > 1:
-            column = in_f.at[e, t, rows_at(halo + p.y * (Z * hub_w), Z * hub_w)]
-            g = group(hub_sems, e, 3, t, column, column, p.y_peers[0][1])
-            for _, where in p.y_peers:
-                g.push(column, column, where)
-            groups["hub", e, 3, t] = g
+        if p.depth:
+            pair_f(e, t, 0)
+        else:
+            column_f(e, t)
+
+    def turn_f(e, t, j):
+        if j >= p.depth:
+            return
+        groups["row", e, j, t].wait_recv()
+        if j + 1 < p.depth:
+            pair_f(e, t, j + 1)
+        else:
+            column_f(e, t)
 
     def take_f(e, t):
         if D > 1:
             groups["halo", e, 1, t].wait_recv()
         if Y > 1:
-            groups["hub", e, 3, t].wait_recv()
+            groups["row", e, p.depth, t].wait_recv()
         return nn(far_ref[...], in_f[e, t])
+
+    def first(turn, e):
+        for t in range(steps):
+            turn(e, t, 0)
+
+    def rest(turn, e):
+        for j in range(1, max(p.depth, 1)):
+            for t in range(steps):
+                turn(e, t, j)
 
     def put_b(e, t, field):
         value = nn(far_t_ref[...], field)
         out_b[e, t] = value.astype(BF16)
-        hub_b[e, t] = value[halo:]
+        hub_b[t] = value[halo:]
 
     def segment(number, base, rows):
         refs = (
@@ -481,10 +567,9 @@
         back = nt(cot_ref[t], mix_ref[2]).astype(BF16)
         back_ref[t] = back
         put_b(0, t, back)
-    ready()
-    for t in range(steps):
+        if t == 0:
+            ready()
         send_hub_b(0, t)
-    for t in range(steps):
         send_halo(0, 0, t)
 
     wide_ref[...] = sig_ref[...].reshape(nodes, (steps + 1) * chans)
@@ -495,24 +580,28 @@
     for t in range(steps):
         both = nn(edge[:, pair[t]], taps_ref[...])
         out_f[0, t] = (jnp.tanh(both[:, :chans]) * jax.nn.sigmoid(both[:, chans:])).astype(BF16)
-    for t in range(steps):
-        turn_hub_b(0, t)
-    for t in range(steps):
         send_hub_f(0, t)
-    for t in range(steps):
-        send_halo(0, 1, t)
-
-    for t in range(steps):
-        back_sum[t] = nt(cot_ref[t], mix_ref[1]) + nn(own_t_ref[...], back_ref[t])
-    for t in range(steps):
+
+    def convolve(t):
         both = nn(wide_ref[:, pair[t]], taps_ref[...])
         tanh_filt = jnp.tanh(both[:, :chans])
         sig_gate = jax.nn.sigmoid(both[:, chans:])
         hidden_ref[t] = (tanh_filt * sig_gate).astype(BF16)
         slope_filt[t] = sig_gate * (1.0 - tanh_filt * tanh_filt)
         slope_gate[t] = tanh_filt * sig_gate * (1.0 - sig_gate)
-    for t in range(steps):
-        turn_hub_f(0, t)
+
+    for t in range(steps):
+        back_sum[t] = nt(cot_ref[t], mix_ref[1]) + nn(own_t_ref[...], back_ref[t])
+    first(turn_b, 0)
+    send_halo(0, 1, 0)
+    for t in range(steps - 1):
+        convolve(t)
+    first(turn_f, 0)
+    rest(turn_b, 0)
+    for t in range(1, steps):
+        send_halo(0, 1, t)
+    convolve(steps - 1)
+    rest(turn_f, 0)
 
     for t in range(steps):
         back = (back_sum[t] + take_b(0, t)).astype(BF16)
@@ -523,20 +612,30 @@
     for t in range(steps):
         hop_sum[t] = nn(own_ref[...], hidden_ref[t])
     for t in range(steps):
-        turn_hub_b(1, t)
+        back_sum[t] = nt(cot_ref[t], mix_ref[0]) + nn(own_t_ref[...], back_one_ref[t])
+    wide_t_ref[...] = wide_ref[...].T
+    first(turn_b, 1)
 
     for t in range(steps):
         hop = (hop_sum[t] + take_f(0, t)).astype(BF16)
         hop_ref[t] = hop
         out_f[1, t] = nn(gather_ref[...], hop).astype(BF16)
         send_hub_f(1, t)
+        if t == 0:
+            send_halo(1, 1, t)
+    rest(turn_b, 1)
+    for t in range(1, steps):
         send_halo(1, 1, t)
 
-    wide_t_ref[...] = wide_ref[...].T
-    for t in range(steps):
-        back_sum[t] = nt(cot_ref[t], mix_ref[0]) + nn(own_t_ref[...], back_one_ref[t])
-    for t in range(steps):
-        turn_hub_f(1, t)
+    for t in range(steps):
+        cot_t_ref[t] = cot_ref[t].T
+    for spot, field in enumerate((hidden_ref, hop_ref)):
+        part = nn(cot_t_ref[0], field[0])
+        for t in range(1, steps):
+            part += nn(cot_t_ref[t], field[t])
+        grads_ref[(4 + spot) * chans : (5 + spot) * chans, :] = part.T
+    mix_seg.core_send()
+    first(turn_f, 1)
 
     for t in range(steps):
         grad_hidden = back_sum[t] + take_b(1, t)
@@ -548,20 +647,14 @@
             outer += nn(wide_t_ref[pair[t], :], held_ref[t, :, span[kind]])
         grads_ref[kind * 2 * chans : (kind + 1) * 2 * chans, :] = outer
         seg.core_send()
-    for t in range(steps):
-        cot_t_ref[t] = cot_ref[t].T
-    for spot, field in enumerate((hidden_ref, hop_ref)):
-        part = nn(cot_t_ref[0], field[0])
-        for t in range(1, steps):
-            part += nn(cot_t_ref[t], field[t])
-        grads_ref[(4 + spot) * chans : (5 + spot) * chans, :] = part.T
+    rest(turn_f, 1)
+    mix_seg.core_take()
+    for t in range(steps):
+        hop_sum[t] = nn(own_ref[...], hop_ref[t])
     filt_seg.core_take()
     gate_seg.core_take()
-    mix_seg.core_send()
-
-    for t in range(steps):
-        hop_sum[t] = nn(own_ref[...], hop_ref[t])
-    mix_seg.core_take()
+    mix_seg.square_take()
+
     part = None
     for t in range(steps):
         hop = (hop_sum[t] + take_f(1, t)).astype(BF16)
@@ -573,7 +666,6 @@
     filt_seg.square_take()
     gate_seg.square_take()
     last_seg.core_take()
-    mix_seg.square_take()
     for t in range(steps):
         layer_ref[t] = (
             wide_ref[:, span[t + 1]].astype(F32)
@@ -592,7 +684,7 @@
         carried = into[:, chans:] + cot_ref[t].astype(F32)
     sgrad_wide[:, span[steps]] = carried.astype(BF16)
     sgrad_ref[...] = sgrad_wide[...].reshape(sgrad_ref.shape)
-    order = (filt_seg, gate_seg, mix_seg, last_seg)
+    order = (mix_seg, filt_seg, gate_seg, last_seg)
     for seg in order:
         seg.line_take(factor)
     for seg in order:
@@ -619,6 +711,15 @@
 
 def shape_of(*dims, dtype=BF16):
     return jax.ShapeDtypeStruct(dims, dtype)
+
+
+def room_for(scratch):
+    sizes = (
+        math.prod(part.shape) * jnp.dtype(part.dtype).itemsize
+        for part in scratch
+        if part.memory_space == pltpu.VMEM
+    )
+    return min(sum(sizes) + (10 << 20), 60 * 1024 * 1024)
 
 
 def body(
@@ -647,7 +748,7 @@
     hw, hub_w = padded(cap), padded(hub_per)
     halo = n_dom * hw
     slots = halo + n_dom * hub_w
-    back_rows = halo + outer * hub_w
+    back_rows = halo + min(outer, 2) * hub_w
     lead_rows = halo + hub_w
     block = tile_vals.shape[1]
     entries = n_dom * cap + hub_rows.size
@@ -656,16 +757,14 @@
     sig = signal.reshape(nodes, hist, chans)
     cot = jnp.transpose(cotangent.reshape(nodes, steps, chans), (1, 0, 2))
 
-    slot = np.arange(halo)
-    expand = (slot[:, None] // hw == np.arange(n_dom)[None, :]).astype(np.float32)
-    lane = (slot % hw).astype(np.int32)[:, None]
-    entry = np.arange(n_dom * cap)
-    halo_place = jnp.asarray(
-        (entry // cap * hw + entry % cap)[:, None] == np.arange(slots)[None, :], dtype=BF16
-    )
-
+    parts = [part[None] for part in (tile_row, tile_col, tile_mask, hub_owner)]
+    parts += [send_rows, send_mask, hub_rows]
+    most = max(part.shape[1] for part in parts)
+    table = jnp.concatenate(
+        [jnp.pad(part, ((0, 0), (0, most - part.shape[1]))) for part in parts]
+    )
     mats = pl.pallas_call(
-        functools.partial(build_kernel, outer, inner),
+        functools.partial(build_kernel, outer, inner, n_dom, hub_w, cap, hub_per),
         out_shape=(
             shape_of(nodes, nodes),
             shape_of(nodes, nodes),
@@ -674,25 +773,22 @@
             shape_of(lead_rows, nodes),
             shape_of(nodes, back_rows),
         ),
-        in_specs=[SMEM] * 3 + [VMEM] + [SMEM] + [VMEM] * 6,
+        in_specs=[HBM] * 2,
         out_specs=(VMEM,) * 6,
         scratch_shapes=[
             pltpu.VMEM((all_tiles, nodes, block), F32),
             pltpu.VMEM((entries, slots), BF16),
+            pltpu.SMEM(table.shape, jnp.int32),
+            pltpu.VMEM(table.shape, jnp.int32),
+            pltpu.VMEM(tile_vals.shape, BF16),
+            pltpu.SemaphoreType.DMA((3,)),
         ],
+        compiler_params=pltpu.CompilerParams(vmem_limit_bytes=BUILD_ROOM),
+        cost_estimate=pl.CostEstimate(flops=3 * 10**9, bytes_accessed=10**7, transcendentals=0),
         name="build",
     )(
-        tile_row,
-        tile_col,
-        tile_mask,
+        table,
         tile_vals,
-        hub_owner,
-        send_rows,
-        send_mask,
-        hub_rows,
-        expand,
-        lane,
-        halo_place,
     )
 
     total_count = nodes * steps * b_dev
@@ -703,8 +799,45 @@
     total = pltpu.VMEM((steps, nodes, chans), F32)
     wide = pltpu.VMEM((nodes, hist * chans), BF16)
     halo_sems = pltpu.SemaphoreType.DMA((2, 2, steps))
-    hub_sems = pltpu.SemaphoreType.DMA((2, 4, steps))
+    hub_sems = pltpu.SemaphoreType.DMA((2, 2 * outer.bit_length(), steps))
     seg_sems = pltpu.SemaphoreType.DMA((4, 5))
+    scratch = [
+        wide,
+        pltpu.VMEM((hist * chans, nodes), BF16),
+        pltpu.VMEM((steps, chans, nodes), BF16),
+        pltpu.VMEM((2 * chans, 2 * chans), BF16),
+        field,
+        field,
+        field,
+        field,
+        total,
+        total,
+        total,
+        total,
+        pltpu.VMEM((steps, nodes, 2 * chans), BF16),
+        wide,
+        pltpu.VMEM((weights, chans), F32),
+        pltpu.VMEM((2, steps, slots, chans), BF16),
+        pltpu.VMEM((steps, n_dom * hub_w, chans), F32),
+        pltpu.VMEM((2, steps, outer * hub_w, chans), BF16),
+        pltpu.VMEM((2, steps, outer * hub_w, chans), F32),
+        pltpu.VMEM((2, steps, outer * hub_w, chans), BF16),
+        pltpu.VMEM((2, steps, outer * hub_w, chans), BF16),
+        pltpu.VMEM((2, steps, back_rows, chans), BF16),
+        pltpu.VMEM((2, steps, lead_rows, chans), BF16),
+        pltpu.VMEM((2, steps, slots, chans), BF16),
+        pltpu.VMEM((weights // pair, chans), F32),
+        pltpu.VMEM((weights // pair, chans), F32),
+        pltpu.VMEM((square, weights // (pair * square), chans), BF16),
+        pltpu.VMEM((square, weights // (pair * square), chans), BF16),
+        pltpu.VMEM((outer, weights // (pair * square), chans), BF16),
+        halo_sems,
+        halo_sems,
+        hub_sems,
+        hub_sems,
+        seg_sems,
+        seg_sems,
+    ]
     layer, sgrad, result = pl.pallas_call(
         functools.partial(
             main_kernel, n_dom, n_batch, hub_w, 1.0 / math.sqrt(total_count)
@@ -716,42 +849,10 @@
         ),
         in_specs=[VMEM] * 10,
         out_specs=(VMEM,) * 3,
-        scratch_shapes=[
-            wide,
-            pltpu.VMEM((hist * chans, nodes), BF16),
-            pltpu.VMEM((steps, chans, nodes), BF16),
-            pltpu.VMEM((2 * chans, 2 * chans), BF16),
-            field,
-            field,
-            field,
-            field,
-            total,
-            total,
-            total,
-            total,
-            pltpu.VMEM((steps, nodes, 2 * chans), BF16),
-            wide,
-            pltpu.VMEM((weights, chans), F32),
-            pltpu.VMEM((2, steps, slots, chans), BF16),
-            pltpu.VMEM((2, steps, n_dom * hub_w, chans), F32),
-            pltpu.VMEM((2, steps, outer * hub_w, chans), BF16),
-            pltpu.VMEM((2, steps, outer * hub_w, chans), BF16),
-            pltpu.VMEM((2, steps, back_rows, chans), BF16),
-            pltpu.VMEM((2, steps, lead_rows, chans), BF16),
-            pltpu.VMEM((2, steps, slots, chans), BF16),
-            pltpu.VMEM((weights // pair, chans), F32),
-            pltpu.VMEM((weights // pair, chans), F32),
-            pltpu.VMEM((square, weights // (pair * square), chans), BF16),
-            pltpu.VMEM((square, weights // (pair * square), chans), BF16),
-            pltpu.VMEM((outer, weights // (pair * square), chans), BF16),
-            halo_sems,
-            halo_sems,
-            hub_sems,
-            hub_sems,
-            seg_sems,
-            seg_sems,
-        ],
-        compiler_params=pltpu.CompilerParams(collective_id=0, has_side_effects=True),
+        scratch_shapes=scratch,
+        compiler_params=pltpu.CompilerParams(
+            collective_id=0, has_side_effects=True, vmem_limit_bytes=room_for(scratch)
+        ),
         name="main",
     )(sig, cot, conv_weight, mix_weight, *mats)
 
@@ -766,6 +867,7 @@
         in_specs=[VMEM] * 3,
         out_specs=(ANY, ANY, VMEM, VMEM),
         scratch_shapes=[pltpu.SemaphoreType.DMA((2,))],
+        compiler_params=pltpu.CompilerParams(vmem_limit_bytes=12 << 20),
         name="finish",
     )(layer, sgrad, result)
     return (

time: 67.7 us -> 59.7 us (0.88)
  Pallas kernels: 66.9 us -> 57 us
  local copies, waits for them, and re-layouts: 0 us -> 1.67 us
    pallas_call x1, Pallas kernels: 59.8 us -> 52.5 us  [body(): pl.pallas_call(functools.partial(main_kernel, n_dom, n_batch, hub_w, 1.0...]
    pallas_call x1, Pallas kernels: 4.2 us -> 2.47 us  [body(): pl.pallas_call(finish_kernel, out_shape=(shape_of(steps, nodes, chans), s...]
    concatenate x0 -> x1, local copies, waits for them, and re-layouts: none -> 0.94 us  [body(): jnp.concatenate([jnp.pad(part, ((0, 0), (0, most - part.shape[1]))) for p...]
    pallas_call x1, Pallas kernels: 2.93 us -> 2.06 us  [body(): pl.pallas_call(functools.partial(build_kernel, outer, inner, n_dom, hub_w...]
    pad x0 -> x1, local copies, waits for them, and re-layouts: none -> 0.69 us  [body(): jnp.pad(part, ((0, 0), (0, most - part.shape[1])))]
where the time goes in v2:
time: 59.7 us; the launch traced here: 59.5 us
  Pallas kernels  57 us (95%)
  local copies, waits for them, and re-layouts  1.67 us (3%)
  between operations  0.78 us (1%)
    pallas_call x1, Pallas kernels, body(): pl.pallas_call(functools.partial(main_kernel, n_dom, n_batch, hub_w, 1.0...  52.5 us
    pallas_call x1, Pallas kernels, body(): pl.pallas_call(finish_kernel, out_shape=(shape_of(steps, nodes, chans), s...  2.47 us
    pallas_call x1, Pallas kernels, body(): pl.pallas_call(functools.partial(build_kernel, outer, inner, n_dom, hub_w...  2.06 us

profile of v2, /device:TPU:0, one launch (start us, length us, event | category | flops | bytes accessed | tf_op | source)
XLA Modules:
  0.0 59.5 jit_solution(13721853992413895265)
XLA Ops:
  0.6 0.0 copy-start.6
  0.6 0.0 copy-start.5
  0.7 0.0 copy-start.4
  0.7 0.0 copy-start.7
  0.7 0.0 copy-start.8
  0.7 0.7 %pad.4 = s32[1,16]{1,0:T(1,128)S(1)} pad(s32[1,8]{1,0:T(1,128)} %bitcast.25, s32[]{:T(128)} %constant.0.clone.1), padding=0_0x0_8 | pad | bytes 100 | tf_op jit(solution)/shard_map/jit(_pad)/pad | solution.py:764
  1.4 0.0 copy-done.6
  1.4 0.0 copy-done.5
  1.4 0.0 copy-done.4
  1.4 0.0 copy-done.7
  1.4 0.0 copy-done.8
  1.4 0.9 %concatenate.3.table_any = s32[28,16]{1,0:T(8,128)S(1)} concatenate(s32[1,16]{1,0:T(1,128)S(1)} %bitcast.18, s32[1,16]{1,0:T(1,128)S(1)} %bitcast.19, s32[1,16]{1,0:T(1,128)} %bitcast.20, s32[1,16]{1,0:T(1,128)S(1)} %pad.4, s32[8,16]{1,0:T(8,128)S(1)} %copy-done.4, s32[8,16]{1,0:T(8,128)S(1)} %copy-done.5, s32[8,16]{1,0:T(8,128)S(1)} %copy-done.6), dimensions={0} | concatenate | bytes 3584 | tf_op jit(solution)/shard_map/concatenate | solution.py:763
  2.4 0.0 copy-start
  2.4 0.0 copy-start.1
  2.4 0.0 copy-start.2
  2.4 0.0 copy-start.3
  2.4 2.1 %build.1 = (bf16[512,512]{1,0:T(8,128)(2,1)S(1)}, bf16[512,512]{1,0:T(8,128)(2,1)S(1)}, bf16[512,256]{1,0:T(8,128)(2,1)S(1)}, bf16[256,512]{1,0:T(8,128)(2,1)S(1...) custom-call(s32[28,16]{1,0:T(8,128)S(1)} %concatenate.3.table_any, bf16[16,128,128]{2,1,0:T(8,128)(2,1)} %tile_any.1), custom_call_target="tpu_custom_call" | custom-call | flops 3000000000 | bytes 10000000 | tf_op jit(solution)/shard_map/build/pallas_call | solution.py:766
  4.5 0.0 copy-done
  4.5 0.0 copy-done.1
  4.5 0.0 copy-done.2
  4.5 0.0 copy-done.3
  4.5 52.5 %main.1 = (bf16[3,512,256]{2,1,0:T(8,128)(2,1)S(1)}, bf16[512,4,256]{2,1,0:T(4,128)(2,1)S(1)}, bf16[1792,256]{1,0:T(8,128)(2,1)S(1)}) custom-call(bf16[512,4,256]{2,1,0:T(4,128)(2,1)S(1)} %bitcast.16, bf16[3,512,256]{2,1,0:T(8,128)(2,1)S(1)} %bitcast.17, bf16[2,2,256,256]{3,2,1,0:T(8,128)(2,1)S(1)} %copy-done.2, bf16[3,256,256]{2,1,0:T(8,128)(2,1)S(1)} %copy-done.3, ...), custom_call_target="tpu_custom_call" | custom-call | tf_op jit(solution)/shard_map/main/pallas_call | solution.py:841
  57.0 2.5 %finish.1 = (bf16[3,512,256]{2,1,0:T(8,128)(2,1)}, bf16[512,4,256]{2,1,0:T(4,128)(2,1)}, f32[1024,256]{1,0:T(8,128)}, f32[768,256]{1,0:T(8,128)}) custom-call(bf16[3,512,256]{2,1,0:T(8,128)(2,1)S(1)} %get-tuple-element.23.layer_ref, bf16[512,4,256]{2,1,0:T(4,128)(2,1)S(1)} %get-tuple-element.24.sgrad_ref, bf16[1792,256]{1,0:T(8,128)(2,1)S(1)} %get-tuple-element.25.result_ref), custom_call_target="tpu_custom_call" | custom-call | tf_op jit(solution)/shard_map/finish/pallas_call | solution.py:859
Async XLA Ops:
  0.6 0.7 %copy-start.6 = (s32[8,16]{1,0:T(8,128)S(1)}, s32[8,16]{1,0:T(8,128)}, u32[]{:S(2)}) copy-start(s32[8,16]{1,0:T(8,128)} %param.23) | copy-start | bytes 1540
  0.6 0.7 %copy-start.5 = (s32[8,16]{1,0:T(8,128)S(1)}, s32[8,16]{1,0:T(8,128)}, u32[]{:S(2)}) copy-start(s32[8,16]{1,0:T(8,128)} %param.17) | copy-start | bytes 1540
  0.7 0.7 %copy-start.4 = (s32[8,16]{1,0:T(8,128)S(1)}, s32[8,16]{1,0:T(8,128)}, u32[]{:S(2)}) copy-start(s32[8,16]{1,0:T(8,128)} %param.16) | copy-start | bytes 1540
  0.7 0.7 %copy-start.7 = (s32[16]{0:T(128)S(1)}, s32[16]{0:T(128)}, u32[]{:S(2)}) copy-start(s32[16]{0:T(128)} %param.19) | copy-start | bytes 196
  0.7 0.7 %copy-start.8 = (s32[16]{0:T(128)S(1)}, s32[16]{0:T(128)}, u32[]{:S(2)}) copy-start(s32[16]{0:T(128)} %param.20) | copy-start | bytes 196
  2.4 2.1 %copy-start = (bf16[512,1,4,256]{3,2,1,0:T(4,128)(2,1)S(1)}, bf16[512,1,4,256]{3,2,1,0:T(4,128)(2,1)}, u32[]{:S(2)}) copy-start(bf16[512,1,4,256]{3,2,1,0:T(4,128)(2,1)} %param.12) | copy-start | bytes 3145732
  2.4 2.1 %copy-start.1 = (bf16[512,1,3,256]{3,0,2,1:T(8,128)(2,1)S(1)}, bf16[512,1,3,256]{3,0,2,1:T(8,128)(2,1)}, u32[]{:S(2)}) copy-start(bf16[512,1,3,256]{3,0,2,1:T(8,128)(2,1)} %param.13) | copy-start | bytes 2359300
  2.4 2.1 %copy-start.2 = (bf16[2,2,256,256]{3,2,1,0:T(8,128)(2,1)S(1)}, bf16[2,2,256,256]{3,2,1,0:T(8,128)(2,1)}, u32[]{:S(2)}) copy-start(bf16[2,2,256,256]{3,2,1,0:T(8,128)(2,1)} %conv_ref.1) | copy-start | bytes 1572868
  2.4 2.1 %copy-start.3 = (bf16[3,256,256]{2,1,0:T(8,128)(2,1)S(1)}, bf16[3,256,256]{2,1,0:T(8,128)(2,1)}, u32[]{:S(2)}) copy-start(bf16[3,256,256]{2,1,0:T(8,128)(2,1)} %mix_ref.1) | copy-start | bytes 1179652

commit v3 on v2

--- a/solution.py
+++ b/solution.py
@@ -153,7 +153,7 @@
     gather_ref[:halo_slots, :] = halo_pick.astype(BF16)
     gather_ref[halo_slots:, :] = hub_pick.astype(BF16)
     scatter_ref[...] = (
-        jnp.concatenate([halo_pick] + [hub_pick] * min(outer, 2), axis=0).T.astype(BF16)
+        jnp.concatenate([halo_pick] + [hub_pick] * outer, axis=0).T.astype(BF16)
     )
 
 
@@ -287,6 +287,90 @@
     def finish(self):
         if self.p.K > 1:
             self.last.wait_recv()
+
+
+class Direct:
+    def __init__(self, place, number, base, rows, refs, trail):
+        self.p, self.base, self.rows, self.trail = place, base, rows, trail
+        self.grads, self.core_in, self.kept, self.out, self.inn, self.result = refs[:6]
+        self.send_sem, self.recv_sem = refs[6].at[number], refs[7].at[number]
+        self.lanes = self.grads.shape[1] // place.K
+        self.piece = rows // len(place.chips)
+        self.half = pl.ds(pl.multiple_of(place.k * self.lanes, 128), self.lanes)
+        self.mine = rows_at(base + place.c * self.piece, self.piece)
+
+    def group(self, stage, sent, landed, where):
+        return Group(
+            self.trail, self.send_sem.at[stage], self.recv_sem.at[stage], sent, landed, where
+        )
+
+    def core_send(self):
+        p = self.p
+        if p.K == 1:
+            return
+        other = pl.ds(pl.multiple_of(p.other_k * self.lanes, 128), self.lanes)
+        self.core = self.group(0, self.core_in, self.core_in, p.partner)
+        self.core.push(
+            self.grads.at[pl.ds(self.base, self.rows), other], self.core_in, p.partner
+        )
+
+    def core_take(self):
+        p = self.p
+        value = self.grads[pl.ds(self.base, self.rows), self.half]
+        if p.K > 1:
+            self.core.wait_recv()
+            value = value + self.core_in[...]
+        self.kept[...] = value
+        self.out[...] = value.astype(BF16)
+        count = len(p.chips)
+        if count > 1:
+            some = self.inn.at[pl.ds(0, (count - 1) * self.piece)]
+            self.chip = self.group(1, some, some, p.chip_peers[0][1])
+            for other, where in p.chip_peers:
+                self.chip.push(
+                    self.out.at[rows_at(other * self.piece, self.piece)],
+                    self.inn.at[rows_at(p.c * self.piece, self.piece)],
+                    where,
+                )
+
+    def chip_take(self, factor):
+        p = self.p
+        value = self.kept[rows_at(p.c * self.piece, self.piece), :]
+        if len(p.chips) > 1:
+            self.chip.wait_recv()
+            for other, _ in p.chip_peers:
+                value = value + self.inn[rows_at(other * self.piece, self.piece), :].astype(F32)
+        self.result[self.mine, self.half] = (value * factor).astype(BF16)
+        if len(p.chips) > 1:
+            rows = pl.ds(self.base, (len(p.chips) - 1) * self.piece)
+            some = self.result.at[rows, self.half]
+            self.spread = self.group(3, some, some, p.chip_peers[0][1])
+            spot = self.result.at[self.mine, self.half]
+            for _, where in p.chip_peers:
+                self.spread.push(spot, spot, where)
+
+    def square_take(self):
+        pass
+
+    def line_take(self, factor):
+        self.chip_take(factor)
+
+    def spread_take(self):
+        p = self.p
+        if len(p.chips) > 1:
+            self.spread.wait_recv()
+        if p.K > 1:
+            spot = self.result.at[pl.ds(self.base, self.rows), self.half]
+            self.last = self.group(4, spot, spot, p.partner)
+            self.last.push(spot, spot, p.partner)
+
+    def finish(self):
+        if self.p.K > 1:
+            self.last.wait_recv()
+
+
+def direct_fits(chips, cores, chans):
+    return chans % (chips * 16) == 0 and chans % (cores * 128) == 0
 
 
 class Place:
@@ -330,11 +414,31 @@
             }
             self.square_peers.append((seat, where))
 
-    def greet(self):
+        self.chips = range(n_dom * self.X)
+        self.c = self.me * self.X + self.x
+        self.chip_peers = []
+        for d in range(1, n_dom * self.X):
+            seat = lax.rem(self.c + d, n_dom * self.X)
+            where = {
+                "dom": lax.div(seat, self.X),
+                "batch": lax.rem(seat, self.X) * self.K + self.k,
+            }
+            self.chip_peers.append((seat, where))
+
+    def greet(self, everyone):
         barrier = pltpu.get_barrier_semaphore()
-        peers = [{"dom": other} for other in self.dom_peers]
+        if everyone:
+            peers = [where for _, where in self.chip_peers]
+        else:
+            peers = [{"dom": other} for other in self.dom_peers] + self.across()
         if self.K > 1:
             peers.append(self.partner)
+        for where in peers:
+            pl.semaphore_signal(barrier, inc=1, device_id=where, device_id_type=MESH)
+        return lambda: pl.semaphore_wait(barrier, len(peers))
+
+    def across(self):
+        peers = []
         for x in range(1, self.X):
             for y in range(self.Y):
                 peers.append(
@@ -343,9 +447,7 @@
                         "dom": self.z * self.Y + lax.rem(self.y + y, self.Y),
                     }
                 )
-        for where in peers:
-            pl.semaphore_signal(barrier, inc=1, device_id=where, device_id_type=MESH)
-        return lambda: pl.semaphore_wait(barrier, len(peers))
+        return peers
 
 
 def main_kernel(
@@ -378,14 +480,13 @@
     slope_gate,
     hop_sum,
     back_sum,
+    layer_sum,
     held_ref,
     sgrad_wide,
     grads_ref,
     out_b,
     hub_b,
     hub_in,
-    hub_sum,
-    hub_land,
     hub_out,
     in_b,
     out_f,
@@ -395,6 +496,10 @@
     square_out,
     square_in,
     z_in,
+    lane_in,
+    lane_kept,
+    lane_out,
+    lane_land,
     halo_send,
     halo_recv,
     hub_send,
@@ -405,7 +510,8 @@
     steps, nodes, chans = cot_ref.shape
     p = Place(n_dom, n_batch)
     D, Z, Y = p.D, p.Z, p.Y
-    ready = p.greet()
+    chans_fit = direct_fits(len(p.chips), p.K, chans)
+    ready = p.greet(chans_fit)
     halo = gather_ref.shape[0] - hub_w
     hw = halo // D
     trail = []
@@ -444,39 +550,24 @@
             )
         groups["hub", e, 0, t] = g
 
-    def pair_b(e, t, i):
-        kept, given, where = p.z_pairs[i]
-        count = hub_w << i
-        spot = rows_at(given * hub_w, count)
-        hub_out[e, t, spot, :] = hub_sum[e, t, spot, :].astype(BF16)
-        if i == 0:
-            land = in_b.at[e, t, pl.ds(halo + hub_w, hub_w)]
-        else:
-            land = hub_land.at[e, t, pl.ds(count, count)]
-        g = group(hub_sems, e, 1 + i, t, land, land, where)
-        g.push(hub_out.at[e, t, spot], land, where)
-        groups["hub", e, 1 + i, t] = g
-
-    def turn_b(e, t, j):
-        if j == 0:
-            value = hub_b[t, rows_at(p.y * (Z * hub_w), Z * hub_w), :]
-            if Y > 1:
-                groups["hub", e, 0, t].wait_recv()
-                value = value + hub_in[e, t].astype(F32)
-            hub_sum[e, t] = value
-        else:
-            i = p.depth - j
-            kept, count = p.z_pairs[i][0], hub_w << i
-            groups["hub", e, 1 + i, t].wait_recv()
-            hub_sum[e, t, rows_at(kept * hub_w, count), :] += hub_land[
-                e, t, pl.ds(count, count), :
-            ].astype(F32)
-        if j < p.depth:
-            pair_b(e, t, p.depth - 1 - j)
-        if j == max(p.depth - 1, 0):
-            in_b[e, t, pl.ds(halo, hub_w), :] = hub_sum[
-                e, t, rows_at(p.seat * hub_w, hub_w), :
-            ].astype(BF16)
+    def turn_b(e, t):
+        value = hub_b[t, rows_at(p.y * (Z * hub_w), Z * hub_w), :]
+        if Y > 1:
+            groups["hub", e, 0, t].wait_recv()
+            value = value + hub_in[e, t].astype(F32)
+        hub_out[e, t] = value.astype(BF16)
+        mine = rows_at(halo + p.z * hub_w, hub_w)
+        if Z > 1:
+            some = in_b.at[e, t, pl.ds(halo, (Z - 1) * hub_w)]
+            g = group(hub_sems, e, 1, t, some, some, p.z_peers[0][1])
+            for seat, where in p.z_peers:
+                g.push(
+                    hub_out.at[e, t, rows_at(flipped(seat, Z) * hub_w, hub_w)],
+                    in_b.at[e, t, mine],
+                    where,
+                )
+            groups["hub", e, 1, t] = g
+        in_b[e, t, mine, :] = hub_out[e, t, rows_at(p.seat * hub_w, hub_w), :]
 
     def take_b(e, t):
         if D > 1:
@@ -491,7 +582,7 @@
         land = in_f.at[e, t, rows_at(base + given * hub_w, count)]
         spot = in_f.at[e, t, rows_at(base + kept * hub_w, count)]
         source = out_f.at[e, t, pl.ds(halo, hub_w)] if i == 0 else spot
-        g = group(hub_sems, e, 1 + p.depth + i, t, land, land, where)
+        g = group(hub_sems, e, 2 + i, t, land, land, where)
         g.push(source, spot, where)
         groups["row", e, i, t] = g
 
@@ -499,7 +590,7 @@
         if Y == 1:
             return
         column = in_f.at[e, t, rows_at(halo + p.y * (Z * hub_w), Z * hub_w)]
-        g = group(hub_sems, e, 1 + 2 * p.depth, t, column, column, p.y_peers[0][1])
+        g = group(hub_sems, e, 2 + p.depth, t, column, column, p.y_peers[0][1])
         for _, where in p.y_peers:
             g.push(column, column, where)
         groups["row", e, p.depth, t] = g
@@ -507,16 +598,22 @@
     def send_hub_f(e, t):
         mine = rows_at(halo + (p.y * Z + p.seat) * hub_w, hub_w)
         in_f[e, t, mine, :] = out_f[e, t, halo:, :]
-        if p.depth:
+        if Z == 1:
+            column_f(e, t)
+        elif e == 0:
             pair_f(e, t, 0)
         else:
-            column_f(e, t)
+            some = in_f.at[e, t, pl.ds(halo, (Z - 1) * hub_w)]
+            g = group(hub_sems, e, 2, t, some, some, p.z_peers[0][1])
+            for _, where in p.z_peers:
+                g.push(out_f.at[e, t, pl.ds(halo, hub_w)], in_f.at[e, t, mine], where)
+            groups["row", e, 0, t] = g
 
     def turn_f(e, t, j):
         if j >= p.depth:
             return
         groups["row", e, j, t].wait_recv()
-        if j + 1 < p.depth:
+        if e == 0 and j + 1 < p.depth:
             pair_f(e, t, j + 1)
         else:
             column_f(e, t)
@@ -528,14 +625,10 @@
             groups["row", e, p.depth, t].wait_recv()
         return nn(far_ref[...], in_f[e, t])
 
-    def first(turn, e):
-        for t in range(steps):
-            turn(e, t, 0)
-
-    def rest(turn, e):
+    def rest_f(e):
         for j in range(1, max(p.depth, 1)):
             for t in range(steps):
-                turn(e, t, j)
+                turn_f(e, t, j)
 
     def put_b(e, t, field):
         value = nn(far_t_ref[...], field)
@@ -556,12 +649,12 @@
         )
         return Segment(p, number, base * chans, rows * chans, refs, trail)
 
-    filt_seg, gate_seg, mix_seg, last_seg = (
-        segment(0, 0, 2),
-        segment(1, 2, 2),
-        segment(2, 4, 2),
-        segment(3, 6, 1),
-    )
+    conv_segs = [segment(i, 2 * i, 2) for i in range(2)]
+    per_kind = len(conv_segs) // 2
+    mix_seg, last_seg = segment(4, 4, 2), segment(5, 6, 1)
+    if chans_fit:
+        refs = (grads_ref, lane_in, lane_kept, lane_out, lane_land, result_ref, seg_send, seg_recv)
+        last_seg = Direct(p, 5, 6 * chans, chans, refs, trail)
 
     for t in range(steps):
         back = nt(cot_ref[t], mix_ref[2]).astype(BF16)
@@ -592,16 +685,14 @@
 
     for t in range(steps):
         back_sum[t] = nt(cot_ref[t], mix_ref[1]) + nn(own_t_ref[...], back_ref[t])
-    first(turn_b, 0)
-    send_halo(0, 1, 0)
-    for t in range(steps - 1):
+    for t in range(steps):
+        turn_b(0, t)
+    for t in range(steps):
+        send_halo(0, 1, t)
+    for t in range(steps):
         convolve(t)
-    first(turn_f, 0)
-    rest(turn_b, 0)
-    for t in range(1, steps):
-        send_halo(0, 1, t)
-    convolve(steps - 1)
-    rest(turn_f, 0)
+    for t in range(steps):
+        turn_f(0, t, 0)
 
     for t in range(steps):
         back = (back_sum[t] + take_b(0, t)).astype(BF16)
@@ -611,69 +702,67 @@
         send_halo(1, 0, t)
     for t in range(steps):
         hop_sum[t] = nn(own_ref[...], hidden_ref[t])
+    rest_f(0)
     for t in range(steps):
         back_sum[t] = nt(cot_ref[t], mix_ref[0]) + nn(own_t_ref[...], back_one_ref[t])
-    wide_t_ref[...] = wide_ref[...].T
-    first(turn_b, 1)
+    for t in range(steps):
+        turn_b(1, t)
+    for t in range(steps):
+        cot_t_ref[t] = cot_ref[t].T
 
     for t in range(steps):
         hop = (hop_sum[t] + take_f(0, t)).astype(BF16)
         hop_ref[t] = hop
         out_f[1, t] = nn(gather_ref[...], hop).astype(BF16)
         send_hub_f(1, t)
-        if t == 0:
-            send_halo(1, 1, t)
-    rest(turn_b, 1)
-    for t in range(1, steps):
+    for t in range(steps):
         send_halo(1, 1, t)
-
-    for t in range(steps):
-        cot_t_ref[t] = cot_ref[t].T
     for spot, field in enumerate((hidden_ref, hop_ref)):
         part = nn(cot_t_ref[0], field[0])
         for t in range(1, steps):
             part += nn(cot_t_ref[t], field[t])
         grads_ref[(4 + spot) * chans : (5 + spot) * chans, :] = part.T
     mix_seg.core_send()
-    first(turn_f, 1)
-
+    wide_t_ref[...] = wide_ref[...].T
+    mix_seg.core_take()
     for t in range(steps):
         grad_hidden = back_sum[t] + take_b(1, t)
-        held_ref[t, :, :chans] = (grad_hidden * slope_filt[t]).astype(BF16)
-        held_ref[t, :, chans:] = (grad_hidden * slope_gate[t]).astype(BF16)
-    for kind, seg in enumerate((filt_seg, gate_seg)):
-        outer = nn(wide_t_ref[pair[0], :], held_ref[0, :, span[kind]])
-        for t in range(1, steps):
-            outer += nn(wide_t_ref[pair[t], :], held_ref[t, :, span[kind]])
-        grads_ref[kind * 2 * chans : (kind + 1) * 2 * chans, :] = outer
-        seg.core_send()
-    rest(turn_f, 1)
-    mix_seg.core_take()
+        for kind, slope in enumerate((slope_filt, slope_gate)):
+            held = (grad_hidden * slope[t]).astype(BF16)
+            held_ref[t, :, span[kind]] = held
+            part = nn(wide_t_ref[pair[t], :], held)
+            rows = slice(kind * 2 * chans, (kind + 1) * 2 * chans)
+            grads_ref[rows, :] = part if t == 0 else grads_ref[rows, :] + part
+            if t == steps - 1:
+                for seg in conv_segs[kind * per_kind : (kind + 1) * per_kind]:
+                    seg.core_send()
     for t in range(steps):
         hop_sum[t] = nn(own_ref[...], hop_ref[t])
-    filt_seg.core_take()
-    gate_seg.core_take()
+    for seg in conv_segs:
+        seg.core_take()
+    for t in range(steps):
+        turn_f(1, t, 0)
     mix_seg.square_take()
+    for t in range(steps):
+        layer_sum[t] = (
+            wide_ref[:, span[t + 1]].astype(F32)
+            + nn(hidden_ref[t], mix_ref[0])
+            + nn(hop_ref[t], mix_ref[1])
+        )
+    for seg in conv_segs:
+        seg.square_take()
 
     part = None
     for t in range(steps):
         hop = (hop_sum[t] + take_f(1, t)).astype(BF16)
-        hop_sum[t] = nn(hop, mix_ref[2])
+        hop_ref[t] = hop
         here = nn(cot_t_ref[t], hop)
         part = here if part is None else part + here
     grads_ref[6 * chans :, :] = part.T
     last_seg.core_send()
-    filt_seg.square_take()
-    gate_seg.square_take()
     last_seg.core_take()
     for t in range(steps):
-        layer_ref[t] = (
-            wide_ref[:, span[t + 1]].astype(F32)
-            + nn(hidden_ref[t], mix_ref[0])
-            + nn(hop_ref[t], mix_ref[1])
-            + hop_sum[t]
-        ).astype(BF16)
-    last_seg.square_take()
+        layer_ref[t] = (layer_sum[t] + nn(hop_ref[t], mix_ref[2])).astype(BF16)
     carried = None
     for t in range(steps):
         into = nt(held_ref[t], taps_ref[...])
@@ -684,12 +773,14 @@
         carried = into[:, chans:] + cot_ref[t].astype(F32)
     sgrad_wide[:, span[steps]] = carried.astype(BF16)
     sgrad_ref[...] = sgrad_wide[...].reshape(sgrad_ref.shape)
-    order = (mix_seg, filt_seg, gate_seg, last_seg)
-    for seg in order:
+    mix_seg.line_take(factor)
+    last_seg.square_take()
+    for seg in conv_segs:
         seg.line_take(factor)
-    for seg in order:
+    last_seg.line_take(factor)
+    for seg in (mix_seg, *conv_segs, last_seg):
         seg.spread_take()
-    for seg in order:
+    for seg in (mix_seg, *conv_segs, last_seg):
         seg.finish()
     for g in trail:
         g.wait_send()
@@ -748,7 +839,7 @@
     hw, hub_w = padded(cap), padded(hub_per)
     halo = n_dom * hw
     slots = halo + n_dom * hub_w
-    back_rows = halo + min(outer, 2) * hub_w
+    back_rows = halo + outer * hub_w
     lead_rows = halo + hub_w
     block = tile_vals.shape[1]
     entries = n_dom * cap + hub_rows.size
@@ -799,8 +890,9 @@
     total = pltpu.VMEM((steps, nodes, chans), F32)
     wide = pltpu.VMEM((nodes, hist * chans), BF16)
     halo_sems = pltpu.SemaphoreType.DMA((2, 2, steps))
-    hub_sems = pltpu.SemaphoreType.DMA((2, 2 * outer.bit_length(), steps))
-    seg_sems = pltpu.SemaphoreType.DMA((4, 5))
+    hub_sems = pltpu.SemaphoreType.DMA((2, 2 + outer.bit_length(), steps))
+    seg_sems = pltpu.SemaphoreType.DMA((6, 5))
+    lanes = [pltpu.VMEM((chans, chans // pair), kind) for kind in (F32, F32, BF16, BF16)]
     scratch = [
         wide,
         pltpu.VMEM((hist * chans, nodes), BF16),
@@ -814,13 +906,12 @@
         total,
         total,
         total,
+        total,
         pltpu.VMEM((steps, nodes, 2 * chans), BF16),
         wide,
         pltpu.VMEM((weights, chans), F32),
         pltpu.VMEM((2, steps, slots, chans), BF16),
         pltpu.VMEM((steps, n_dom * hub_w, chans), F32),
-        pltpu.VMEM((2, steps, outer * hub_w, chans), BF16),
-        pltpu.VMEM((2, steps, outer * hub_w, chans), F32),
         pltpu.VMEM((2, steps, outer * hub_w, chans), BF16),
         pltpu.VMEM((2, steps, outer * hub_w, chans), BF16),
         pltpu.VMEM((2, steps, back_rows, chans), BF16),
@@ -831,6 +922,7 @@
         pltpu.VMEM((square, weights // (pair * square), chans), BF16),
         pltpu.VMEM((square, weights // (pair * square), chans), BF16),
         pltpu.VMEM((outer, weights // (pair * square), chans), BF16),
+        *lanes,
         halo_sems,
         halo_sems,
         hub_sems,

time: 59.7 us -> 58.3 us (0.977)
  Pallas kernels: 57 us -> 55.6 us
    pallas_call x1, Pallas kernels: 52.5 us -> 51.1 us  [body(): pl.pallas_call(functools.partial(main_kernel, n_dom, n_batch, hub_w, 1.0...]
where the time goes in v3:
time: 58.3 us; the launch traced here: 58.1 us
  Pallas kernels  55.6 us (95%)
  local copies, waits for them, and re-layouts  1.67 us (3%)
  between operations  0.78 us (1%)
    pallas_call x1, Pallas kernels, body(): pl.pallas_call(functools.partial(main_kernel, n_dom, n_batch, hub_w, 1.0...  51.1 us
    pallas_call x1, Pallas kernels, body(): pl.pallas_call(finish_kernel, out_shape=(shape_of(steps, nodes, chans), s...  2.47 us
    pallas_call x1, Pallas kernels, body(): pl.pallas_call(functools.partial(build_kernel, outer, inner, n_dom, hub_w...  2.06 us

profile of v3, /device:TPU:0, one launch (start us, length us, event | category | flops | bytes accessed | tf_op | source)
XLA Modules:
  0.0 58.1 jit_solution(1907406054930976025)
XLA Ops:
  0.6 0.0 copy-start.6
  0.6 0.0 copy-start.5
  0.7 0.0 copy-start.4
  0.7 0.0 copy-start.7
  0.7 0.0 copy-start.8
  0.7 0.7 %pad.4 = s32[1,16]{1,0:T(1,128)S(1)} pad(s32[1,8]{1,0:T(1,128)} %bitcast.25, s32[]{:T(128)} %constant.0.clone.1), padding=0_0x0_8 | pad | bytes 100 | tf_op jit(solution)/shard_map/jit(_pad)/pad | solution.py:855
  1.4 0.0 copy-done.6
  1.4 0.0 copy-done.5
  1.4 0.0 copy-done.4
  1.4 0.0 copy-done.7
  1.4 0.0 copy-done.8
  1.4 0.9 %concatenate.3.table_any = s32[28,16]{1,0:T(8,128)S(1)} concatenate(s32[1,16]{1,0:T(1,128)S(1)} %bitcast.18, s32[1,16]{1,0:T(1,128)S(1)} %bitcast.19, s32[1,16]{1,0:T(1,128)} %bitcast.20, s32[1,16]{1,0:T(1,128)S(1)} %pad.4, s32[8,16]{1,0:T(8,128)S(1)} %copy-done.4, s32[8,16]{1,0:T(8,128)S(1)} %copy-done.5, s32[8,16]{1,0:T(8,128)S(1)} %copy-done.6), dimensions={0} | concatenate | bytes 3584 | tf_op jit(solution)/shard_map/concatenate | solution.py:854
  2.4 0.0 copy-start
  2.4 0.0 copy-start.1
  2.4 0.0 copy-start.2
  2.4 0.0 copy-start.3
  2.4 2.1 %build.1 = (bf16[512,512]{1,0:T(8,128)(2,1)S(1)}, bf16[512,512]{1,0:T(8,128)(2,1)S(1)}, bf16[512,256]{1,0:T(8,128)(2,1)S(1)}, bf16[256,512]{1,0:T(8,128)(2,1)S(1...) custom-call(s32[28,16]{1,0:T(8,128)S(1)} %concatenate.3.table_any, bf16[16,128,128]{2,1,0:T(8,128)(2,1)} %tile_any.1), custom_call_target="tpu_custom_call" | custom-call | flops 3000000000 | bytes 10000000 | tf_op jit(solution)/shard_map/build/pallas_call | solution.py:857
  4.5 0.0 copy-done
  4.5 0.0 copy-done.1
  4.5 0.0 copy-done.2
  4.5 0.0 copy-done.3
  4.5 51.1 %main.1 = (bf16[3,512,256]{2,1,0:T(8,128)(2,1)S(1)}, bf16[512,4,256]{2,1,0:T(4,128)(2,1)S(1)}, bf16[1792,256]{1,0:T(8,128)(2,1)S(1)}) custom-call(bf16[512,4,256]{2,1,0:T(4,128)(2,1)S(1)} %bitcast.16, bf16[3,512,256]{2,1,0:T(8,128)(2,1)S(1)} %bitcast.17, bf16[2,2,256,256]{3,2,1,0:T(8,128)(2,1)S(1)} %copy-done.2, bf16[3,256,256]{2,1,0:T(8,128)(2,1)S(1)} %copy-done.3, ...), custom_call_target="tpu_custom_call" | custom-call | tf_op jit(solution)/shard_map/main/pallas_call | solution.py:933
  55.6 2.5 %finish.1 = (bf16[3,512,256]{2,1,0:T(8,128)(2,1)}, bf16[512,4,256]{2,1,0:T(4,128)(2,1)}, f32[1024,256]{1,0:T(8,128)}, f32[768,256]{1,0:T(8,128)}) custom-call(bf16[3,512,256]{2,1,0:T(8,128)(2,1)S(1)} %get-tuple-element.23.layer_ref, bf16[512,4,256]{2,1,0:T(4,128)(2,1)S(1)} %get-tuple-element.24.sgrad_ref, bf16[1792,256]{1,0:T(8,128)(2,1)S(1)} %get-tuple-element.25.result_ref), custom_call_target="tpu_custom_call" | custom-call | tf_op jit(solution)/shard_map/finish/pallas_call | solution.py:951
Async XLA Ops:
  0.6 0.7 %copy-start.6 = (s32[8,16]{1,0:T(8,128)S(1)}, s32[8,16]{1,0:T(8,128)}, u32[]{:S(2)}) copy-start(s32[8,16]{1,0:T(8,128)} %param.23) | copy-start | bytes 1540
  0.6 0.7 %copy-start.5 = (s32[8,16]{1,0:T(8,128)S(1)}, s32[8,16]{1,0:T(8,128)}, u32[]{:S(2)}) copy-start(s32[8,16]{1,0:T(8,128)} %param.17) | copy-start | bytes 1540
  0.7 0.7 %copy-start.4 = (s32[8,16]{1,0:T(8,128)S(1)}, s32[8,16]{1,0:T(8,128)}, u32[]{:S(2)}) copy-start(s32[8,16]{1,0:T(8,128)} %param.16) | copy-start | bytes 1540
  0.7 0.7 %copy-start.7 = (s32[16]{0:T(128)S(1)}, s32[16]{0:T(128)}, u32[]{:S(2)}) copy-start(s32[16]{0:T(128)} %param.19) | copy-start | bytes 196
  0.7 0.7 %copy-start.8 = (s32[16]{0:T(128)S(1)}, s32[16]{0:T(128)}, u32[]{:S(2)}) copy-start(s32[16]{0:T(128)} %param.20) | copy-start | bytes 196
  2.4 2.1 %copy-start = (bf16[512,1,4,256]{3,2,1,0:T(4,128)(2,1)S(1)}, bf16[512,1,4,256]{3,2,1,0:T(4,128)(2,1)}, u32[]{:S(2)}) copy-start(bf16[512,1,4,256]{3,2,1,0:T(4,128)(2,1)} %param.12) | copy-start | bytes 3145732
  2.4 2.1 %copy-start.1 = (bf16[512,1,3,256]{3,0,2,1:T(8,128)(2,1)S(1)}, bf16[512,1,3,256]{3,0,2,1:T(8,128)(2,1)}, u32[]{:S(2)}) copy-start(bf16[512,1,3,256]{3,0,2,1:T(8,128)(2,1)} %param.13) | copy-start | bytes 2359300
  2.4 2.1 %copy-start.2 = (bf16[2,2,256,256]{3,2,1,0:T(8,128)(2,1)S(1)}, bf16[2,2,256,256]{3,2,1,0:T(8,128)(2,1)}, u32[]{:S(2)}) copy-start(bf16[2,2,256,256]{3,2,1,0:T(8,128)(2,1)} %conv_ref.1) | copy-start | bytes 1572868
  2.4 2.1 %copy-start.3 = (bf16[3,256,256]{2,1,0:T(8,128)(2,1)S(1)}, bf16[3,256,256]{2,1,0:T(8,128)(2,1)}, u32[]{:S(2)}) copy-start(bf16[3,256,256]{2,1,0:T(8,128)(2,1)} %mix_ref.1) | copy-start | bytes 1179652

commit v4 on v3

--- a/solution.py
+++ b/solution.py
@@ -97,15 +97,8 @@
     source = lax.div(lax.broadcasted_iota(jnp.int32, (halo_slots, n_dom), 0), halo_width)
     expand = (source == lax.broadcasted_iota(jnp.int32, (halo_slots, n_dom), 1)).astype(F32)
     lane = lax.rem(lax.broadcasted_iota(jnp.int32, (halo_slots, cap), 0), halo_width)
-    for load in loads:
+    for load in loads[:-1]:
         load.wait()
-    for t in range(tiles):
-
-        @pl.when(ints_ref[2, t] == 1)
-        def _():
-            rows = pl.ds(pl.multiple_of(ints_ref[0, t] * block, block), block)
-            dense_ref[ints_ref[1, t], rows, :] += tile_ref[t].astype(F32)
-
     slot = lax.broadcasted_iota(jnp.int32, (hub_per, slots), 1)
     entry = lax.broadcasted_iota(jnp.int32, (hub_per, slots), 0) + halo_slots
     me = lax.axis_index("dom")
@@ -119,17 +112,6 @@
         ).astype(BF16)
         owned = (owner == me).astype(F32)
         hub += owned * (hubs_ref[o : o + 1, :hub_per].astype(F32) + 1.0)
-    far = nn(dense_ref[own_tiles].astype(BF16), place_ref[:block, :])
-    for c in range(own_tiles + 1, all_tiles):
-        at = (c - own_tiles) * block
-        far += nn(dense_ref[c].astype(BF16), place_ref[at : at + block, :])
-    far_ref[...] = far.astype(BF16)
-    far_t_ref[...] = far.T.astype(BF16)
-    for c in range(own_tiles):
-        part = dense_ref[c]
-        own_ref[:, c * block : (c + 1) * block] = part.astype(BF16)
-        own_t_ref[c * block : (c + 1) * block, :] = part.T.astype(BF16)
-
     chosen = jnp.where(flag_ref[:, :cap] == 1, rows_ref[:, :cap].astype(F32) + 1.0, 0.0)
     spread = jnp.dot(
         expand, chosen, precision=lax.Precision.HIGHEST, preferred_element_type=F32
@@ -155,6 +137,24 @@
     scatter_ref[...] = (
         jnp.concatenate([halo_pick] + [hub_pick] * outer, axis=0).T.astype(BF16)
     )
+    loads[-1].wait()
+    for t in range(tiles):
+
+        @pl.when(ints_ref[2, t] == 1)
+        def _():
+            rows = pl.ds(pl.multiple_of(ints_ref[0, t] * block, block), block)
+            dense_ref[ints_ref[1, t], rows, :] += tile_ref[t].astype(F32)
+
+    far = nn(dense_ref[own_tiles].astype(BF16), place_ref[:block, :])
+    for c in range(own_tiles + 1, all_tiles):
+        at = (c - own_tiles) * block
+        far += nn(dense_ref[c].astype(BF16), place_ref[at : at + block, :])
+    far_ref[...] = far.astype(BF16)
+    far_t_ref[...] = far.T.astype(BF16)
+    for c in range(own_tiles):
+        part = dense_ref[c]
+        own_ref[:, c * block : (c + 1) * block] = part.astype(BF16)
+        own_t_ref[c * block : (c + 1) * block, :] = part.T.astype(BF16)
 
 
 def rows_at(start, count):
@@ -699,6 +699,7 @@
         back_one_ref[t] = back
         put_b(1, t, back)
         send_hub_b(1, t)
+    for t in range(steps):
         send_halo(1, 0, t)
     for t in range(steps):
         hop_sum[t] = nn(own_ref[...], hidden_ref[t])
@@ -773,12 +774,10 @@
         carried = into[:, chans:] + cot_ref[t].astype(F32)
     sgrad_wide[:, span[steps]] = carried.astype(BF16)
     sgrad_ref[...] = sgrad_wide[...].reshape(sgrad_ref.shape)
-    mix_seg.line_take(factor)
     last_seg.square_take()
-    for seg in conv_segs:
+    for seg in (*conv_segs, mix_seg, last_seg):
         seg.line_take(factor)
-    last_seg.line_take(factor)
-    for seg in (mix_seg, *conv_segs, last_seg):
+    for seg in (*conv_segs, mix_seg, last_seg):
         seg.spread_take()
     for seg in (mix_seg, *conv_segs, last_seg):
         seg.finish()
@@ -786,16 +785,24 @@
         g.wait_send()
 
 
-def finish_kernel(layer_ref, sgrad_ref, result_ref, layer_out, sgrad_out, conv_out, mix_out, sems):
-    copies = [
-        pltpu.make_async_copy(layer_ref, layer_out, sems.at[0]),
-        pltpu.make_async_copy(sgrad_ref, sgrad_out, sems.at[1]),
-    ]
-    for copy in copies:
+def finish_kernel(
+    layer_ref, sgrad_ref, result_ref, layer_out, sgrad_out, conv_out, mix_out, stage, sems
+):
+    chans = result_ref.shape[1]
+    copies = []
+
+    def send(source, target):
+        copy = pltpu.make_async_copy(source, target, sems.at[len(copies)])
         copy.start()
-    rows = conv_out.shape[0]
-    conv_out[...] = result_ref[:rows, :].astype(F32)
-    mix_out[...] = result_ref[rows:, :].astype(F32)
+        copies.append(copy)
+
+    send(layer_ref, layer_out)
+    send(sgrad_ref, sgrad_out)
+    for base, out in ((0, conv_out), (conv_out.shape[0], mix_out)):
+        for at in range(0, out.shape[0], chans):
+            rows = pl.ds(base + at, chans)
+            stage[rows, :] = result_ref[rows, :].astype(F32)
+            send(stage.at[rows], out.at[pl.ds(at, chans)])
     for copy in copies:
         copy.wait()
 
@@ -957,8 +964,8 @@
             shape_of(3 * chans, chans, dtype=F32),
         ),
         in_specs=[VMEM] * 3,
-        out_specs=(ANY, ANY, VMEM, VMEM),
-        scratch_shapes=[pltpu.SemaphoreType.DMA((2,))],
+        out_specs=(ANY,) * 4,
+        scratch_shapes=[pltpu.VMEM((weights, chans), F32), pltpu.SemaphoreType.DMA((9,))],
         compiler_params=pltpu.CompilerParams(vmem_limit_bytes=12 << 20),
         name="finish",
     )(layer, sgrad, result)

time: 58.3 us -> 57.1 us (0.979)
  Pallas kernels: 55.6 us -> 54.5 us
where the time goes in v4:
time: 57.1 us; the launch traced here: 56.9 us
  Pallas kernels  54.5 us (95%)
  local copies, waits for them, and re-layouts  1.67 us (3%)
  between operations  0.78 us (1%)
    pallas_call x1, Pallas kernels, body(): pl.pallas_call(functools.partial(main_kernel, n_dom, n_batch, hub_w, 1.0...  50.7 us
    pallas_call x1, Pallas kernels, body(): pl.pallas_call(functools.partial(build_kernel, outer, inner, n_dom, hub_w...  1.91 us
    pallas_call x1, Pallas kernels, body(): pl.pallas_call(finish_kernel, out_shape=(shape_of(steps, nodes, chans), s...  1.9 us

profile of v4, /device:TPU:0, one launch (start us, length us, event | category | flops | bytes accessed | tf_op | source)
XLA Modules:
  0.0 56.9 jit_solution(17047780711533554682)
XLA Ops:
  0.6 0.0 copy-start.6
  0.6 0.0 copy-start.5
  0.7 0.0 copy-start.4
  0.7 0.0 copy-start.7
  0.7 0.0 copy-start.8
  0.7 0.7 %pad.4 = s32[1,16]{1,0:T(1,128)S(1)} pad(s32[1,8]{1,0:T(1,128)} %bitcast.25, s32[]{:T(128)} %constant.0.clone.1), padding=0_0x0_8 | pad | bytes 100 | tf_op jit(solution)/shard_map/jit(_pad)/pad | solution.py:862
  1.4 0.0 copy-done.6
  1.4 0.0 copy-done.5
  1.4 0.0 copy-done.4
  1.4 0.0 copy-done.7
  1.4 0.0 copy-done.8
  1.4 0.9 %concatenate.3.table_any = s32[28,16]{1,0:T(8,128)S(1)} concatenate(s32[1,16]{1,0:T(1,128)S(1)} %bitcast.18, s32[1,16]{1,0:T(1,128)S(1)} %bitcast.19, s32[1,16]{1,0:T(1,128)} %bitcast.20, s32[1,16]{1,0:T(1,128)S(1)} %pad.4, s32[8,16]{1,0:T(8,128)S(1)} %copy-done.4, s32[8,16]{1,0:T(8,128)S(1)} %copy-done.5, s32[8,16]{1,0:T(8,128)S(1)} %copy-done.6), dimensions={0} | concatenate | bytes 3584 | tf_op jit(solution)/shard_map/concatenate | solution.py:861
  2.4 0.0 copy-start
  2.4 0.0 copy-start.1
  2.4 0.0 copy-start.2
  2.4 0.0 copy-start.3
  2.4 1.9 %build.1 = (bf16[512,512]{1,0:T(8,128)(2,1)S(1)}, bf16[512,512]{1,0:T(8,128)(2,1)S(1)}, bf16[512,256]{1,0:T(8,128)(2,1)S(1)}, bf16[256,512]{1,0:T(8,128)(2,1)S(1...) custom-call(s32[28,16]{1,0:T(8,128)S(1)} %concatenate.3.table_any, bf16[16,128,128]{2,1,0:T(8,128)(2,1)} %tile_any.1), custom_call_target="tpu_custom_call" | custom-call | flops 3000000000 | bytes 10000000 | tf_op jit(solution)/shard_map/build/pallas_call | solution.py:864
  4.3 0.0 copy-done
  4.3 0.0 copy-done.1
  4.3 0.0 copy-done.2
  4.3 0.0 copy-done.3
  4.4 50.7 %main.1 = (bf16[3,512,256]{2,1,0:T(8,128)(2,1)S(1)}, bf16[512,4,256]{2,1,0:T(4,128)(2,1)S(1)}, bf16[1792,256]{1,0:T(8,128)(2,1)S(1)}) custom-call(bf16[512,4,256]{2,1,0:T(4,128)(2,1)S(1)} %bitcast.16, bf16[3,512,256]{2,1,0:T(8,128)(2,1)S(1)} %bitcast.17, bf16[2,2,256,256]{3,2,1,0:T(8,128)(2,1)S(1)} %copy-done.2, bf16[3,256,256]{2,1,0:T(8,128)(2,1)S(1)} %copy-done.3, ...), custom_call_target="tpu_custom_call" | custom-call | tf_op jit(solution)/shard_map/main/pallas_call | solution.py:940
  55.0 1.9 %finish.1 = (bf16[3,512,256]{2,1,0:T(8,128)(2,1)}, bf16[512,4,256]{2,1,0:T(4,128)(2,1)}, f32[1024,256]{1,0:T(8,128)}, f32[768,256]{1,0:T(8,128)}) custom-call(bf16[3,512,256]{2,1,0:T(8,128)(2,1)S(1)} %get-tuple-element.23.layer_ref, bf16[512,4,256]{2,1,0:T(4,128)(2,1)S(1)} %get-tuple-element.24.sgrad_ref, bf16[1792,256]{1,0:T(8,128)(2,1)S(1)} %get-tuple-element.25.result_ref), custom_call_target="tpu_custom_call" | custom-call | tf_op jit(solution)/shard_map/finish/pallas_call | solution.py:958
Async XLA Ops:
  0.6 0.7 %copy-start.6 = (s32[8,16]{1,0:T(8,128)S(1)}, s32[8,16]{1,0:T(8,128)}, u32[]{:S(2)}) copy-start(s32[8,16]{1,0:T(8,128)} %param.23) | copy-start | bytes 1540
  0.6 0.7 %copy-start.5 = (s32[8,16]{1,0:T(8,128)S(1)}, s32[8,16]{1,0:T(8,128)}, u32[]{:S(2)}) copy-start(s32[8,16]{1,0:T(8,128)} %param.17) | copy-start | bytes 1540
  0.7 0.7 %copy-start.4 = (s32[8,16]{1,0:T(8,128)S(1)}, s32[8,16]{1,0:T(8,128)}, u32[]{:S(2)}) copy-start(s32[8,16]{1,0:T(8,128)} %param.16) | copy-start | bytes 1540
  0.7 0.7 %copy-start.7 = (s32[16]{0:T(128)S(1)}, s32[16]{0:T(128)}, u32[]{:S(2)}) copy-start(s32[16]{0:T(128)} %param.19) | copy-start | bytes 196
  0.7 0.7 %copy-start.8 = (s32[16]{0:T(128)S(1)}, s32[16]{0:T(128)}, u32[]{:S(2)}) copy-start(s32[16]{0:T(128)} %param.20) | copy-start | bytes 196
  2.4 2.0 %copy-start = (bf16[512,1,4,256]{3,2,1,0:T(4,128)(2,1)S(1)}, bf16[512,1,4,256]{3,2,1,0:T(4,128)(2,1)}, u32[]{:S(2)}) copy-start(bf16[512,1,4,256]{3,2,1,0:T(4,128)(2,1)} %param.12) | copy-start | bytes 3145732
  2.4 2.0 %copy-start.1 = (bf16[512,1,3,256]{3,0,2,1:T(8,128)(2,1)S(1)}, bf16[512,1,3,256]{3,0,2,1:T(8,128)(2,1)}, u32[]{:S(2)}) copy-start(bf16[512,1,3,256]{3,0,2,1:T(8,128)(2,1)} %param.13) | copy-start | bytes 2359300
  2.4 2.0 %copy-start.2 = (bf16[2,2,256,256]{3,2,1,0:T(8,128)(2,1)S(1)}, bf16[2,2,256,256]{3,2,1,0:T(8,128)(2,1)}, u32[]{:S(2)}) copy-start(bf16[2,2,256,256]{3,2,1,0:T(8,128)(2,1)} %conv_ref.1) | copy-start | bytes 1572868
  2.4 2.0 %copy-start.3 = (bf16[3,256,256]{2,1,0:T(8,128)(2,1)S(1)}, bf16[3,256,256]{2,1,0:T(8,128)(2,1)}, u32[]{:S(2)}) copy-start(bf16[3,256,256]{2,1,0:T(8,128)(2,1)} %mix_ref.1) | copy-start | bytes 1179652
